TPU v7x, 256 devices: a whole 4x4x8 slice. The times are simulated.
256 devices in a mesh: gx: 32 (over z, x), gy: 8 (over y, core).
Axes of the slice: x: 4, y: 4, z: 8, core: 2. Of those that a mesh axis runs over, the one named last changes fastest.
Arguments:
- krylov_block: float32 [16, 26, 256, 2048], P(None, None, 'gx', 'gy'), may hold values from -13 to 13
- prior_basis: float32 [24, 26, 256, 2048], P(None, None, 'gx', 'gy'), may hold values from -5.2 to 5.2
- flux_along: float32 [26, 26], replicated, may hold values from -1.25 to 1.25
- flux_across: float32 [26, 26], replicated, may hold values from -1.25 to 1.25
- collision: float32 [256, 2048], P('gx', 'gy'), may hold values from 1 to 10
- field_rates: float32 [26], replicated, may hold values from 0.5 to 2
- wall_table: float32 [4, 26], replicated, may hold values from 0.5 to 3
- wall_mask: int32 [256, 2048], P('gx', 'gy'), may hold values 0 or 1
- wall_type: int32 [256, 2048], P('gx', 'gy'), may hold values from 0 to 3
Outputs:
- new_block: float32 [16, 26, 256, 2048], P(None, None, 'gx', 'gy')
- projection: float32 [24, 16], replicated
- triangle: float32 [16, 16], replicated
All inputs are finite; a program needn't handle non-finite values. No bound on the sum of `wall_mask` on one device may be relied on, other than what follows from the above.
Results may differ from a plain program's by a relative error of at most 0.0003.
Values sent between devices are 32-bit elements; how exact they have to be, the bound alone decides.
No kernel may reach another device: no remote copies, remote signals or barrier semaphores. Data moves between devices by JAX's collectives and lax.ppermute only.
A program may use at most 128 MiB of HBM per device.

v0:
```python
import functools

import jax
import jax.numpy as jnp
from jax import lax
from jax.experimental import pallas as pl
from jax.experimental.pallas import tpu as pltpu
from jax.sharding import Mesh
from jax.sharding import PartitionSpec as P

GX = ("gx_z", "gx_x")
GY = ("gy_y", "gy_c")
STAGES = (("gx_x", "gy_y"), ("gx_z", "gy_c"))

DAMP = 0.0625
PRECISE = lax.Precision.HIGHEST
F32 = jnp.float32
BF16 = jnp.bfloat16

M = 16
K = 24
F = 26
X = 8
Y = 256
FX = F * X
MX = M * X
KX = K * X
PAIRS = M // 2
HALO = 4 * F

NN = (((1,), (0,)), ((), ()))
NT = (((1,), (1,)), ((), ()))
TN = (((0,), (0,)), ((), ()))


def exact_dot(a, b, dims=NN):
    return lax.dot_general(a, b, dims, precision=PRECISE, preferred_element_type=F32)


def half_dot(a, b, dims=NN):
    return lax.dot_general(a, b, dims, preferred_element_type=F32)


def split2(v):
    hi = v.astype(BF16)
    return hi, (v - hi.astype(F32)).astype(BF16)


def split3(v):
    hi = v.astype(BF16)
    rest = v - hi.astype(F32)
    mid = rest.astype(BF16)
    return hi, mid, (rest - mid.astype(F32)).astype(BF16)


def iota(shape, dim):
    return lax.broadcasted_iota(jnp.int32, shape, dim)


def where0(mask, v):
    return jnp.where(mask, v, jnp.zeros_like(v))


def spread(small, rows, cols):
    n, k = small.shape
    left = (iota((rows, n), 0) // X == iota((rows, n), 1)).astype(F32)
    right = (iota((k, cols), 1) // X == iota((k, cols), 0)).astype(F32)
    return exact_dot(exact_dot(left, small), right)


def two_sum(a, b):
    s = a + b
    t = s - a
    return s, (a - (s - t)) + (b - t)


def roll(v, shift, axis):
    size = v.shape[axis]
    return pltpu.roll(v, shift % size if isinstance(shift, int) else shift, axis)


def pack_kernel(v_ref, first_ref, last_ref, yfirst_ref, ylast_ref, *, step_m):
    step = pl.program_id(0)
    for i in range(step_m):
        for f in range(F):
            at = (i % 2 * F + f) * 2
            first_ref[i // 2, at : at + 2, :] = v_ref[i, f, 0:2, :]
            last_ref[i // 2, at : at + 2, :] = v_ref[i, f, X - 2 : X, :]
    lane = iota((FX, 128), 1)
    at_first, at_last = yfirst_ref[...], ylast_ref[...]
    for i in range(step_m):
        m = step * step_m + i
        mine = lane // 2 == m
        left = v_ref[i, :, :, 0:128].reshape(FX, 128)
        right = v_ref[i, :, :, Y - 128 : Y].reshape(FX, 128)
        at_first = jnp.where(mine, roll(left, 2 * m, 1), at_first)
        at_last = jnp.where(mine, roll(right, 2 * m + 2, 1), at_last)
    keep = lane < 2 * step_m * (step + 1)
    yfirst_ref[...] = where0(keep, at_first)
    ylast_ref[...] = where0(keep, at_last)


def pack(v, step_m=4):
    return pl.pallas_call(
        functools.partial(pack_kernel, step_m=step_m),
        grid=(M // step_m,),
        in_specs=[pl.BlockSpec((step_m, F, X, Y), lambda i: (i, 0, 0, 0))],
        out_specs=[
            pl.BlockSpec((step_m // 2, HALO, Y), lambda i: (i, 0, 0)),
            pl.BlockSpec((step_m // 2, HALO, Y), lambda i: (i, 0, 0)),
            pl.BlockSpec((FX, 128), lambda i: (0, 0)),
            pl.BlockSpec((FX, 128), lambda i: (0, 0)),
        ],
        out_shape=[
            jax.ShapeDtypeStruct((PAIRS, HALO, Y), F32),
            jax.ShapeDtypeStruct((PAIRS, HALO, Y), F32),
            jax.ShapeDtypeStruct((FX, 128), F32),
            jax.ShapeDtypeStruct((FX, 128), F32),
        ],
        cost_estimate=pl.CostEstimate(flops=10**6, bytes_accessed=6 * 10**6, transcendentals=0),
        name="pack",
    )(v)


def inside_kernel(
    v_ref, along_ref, across_ref, coll_ref, mask_ref, type_ref, rate_ref, table_ref,
    out_ref, w_hi, w_lo, coeff, *, step_m,
):
    @pl.when(pl.program_id(0) == 0)
    def _():
        row, col = iota((FX, FX), 0), iota((FX, FX), 1)
        same_f = row // X == col // X
        step = col % X - row % X
        fa = spread(along_ref[...], FX, FX)
        fc = spread(across_ref[...], FX, FX)
        wx = where0(step == 1, 0.5 * fa) - where0(step == -1, 0.5 * fa)
        near = same_f & (jnp.abs(step) == 1)
        far = same_f & (jnp.abs(step) == 2)
        wx = wx + jnp.where(near, -4.0 * DAMP, 0.0) + jnp.where(far, DAMP, 0.0)
        wy = where0(step == 0, 0.5 * fc)
        hi, lo = split2(wx)
        w_hi[0:FX, :] = hi
        w_lo[0:FX, :] = lo
        hi, lo = split2(wy)
        w_hi[FX : 2 * FX, :] = hi
        w_lo[FX : 2 * FX, :] = lo
        walls = [
            jnp.where(type_ref[...] == t, mask_ref[...].astype(F32), 0.0)
            for t in range(table_ref.shape[0])
        ]
        for f in range(F):
            c = coll_ref[...] * rate_ref[f]
            for t, wall in enumerate(walls):
                c = c + wall * table_ref[t, f]
            coeff[f * X : (f + 1) * X, :] = c + 12.0 * DAMP

    lane = iota((FX, Y), 1)

    def one(i, carry):
        v = v_ref[i].reshape(FX, Y)
        hi, lo = split2(v)
        both = half_dot(w_hi[...], hi) + half_dot(w_lo[...], hi) + half_dot(w_hi[...], lo)
        u = both[FX:]
        out = both[:FX] + coeff[...] * v
        side = 4.0 * DAMP * v
        out = out + where0(lane < Y - 1, roll(u - side, -1, 1))
        out = out - where0(lane > 0, roll(u + side, 1, 1))
        two = DAMP * v
        out = out + where0(lane < Y - 2, roll(two, -2, 1)) + where0(lane > 1, roll(two, 2, 1))
        out_ref[i] = out.reshape(F, X, Y)
        return carry

    lax.fori_loop(0, step_m, one, 0)


def inside(v, along, across, coll, mask, types, rates, table, step_m=4):
    smem = pl.BlockSpec(memory_space=pltpu.SMEM)
    whole2 = lambda i: (0, 0)
    return pl.pallas_call(
        functools.partial(inside_kernel, step_m=step_m),
        grid=(M // step_m,),
        in_specs=[
            pl.BlockSpec((step_m, F, X, Y), lambda i: (i, 0, 0, 0)),
            pl.BlockSpec((F, F), whole2),
            pl.BlockSpec((F, F), whole2),
            pl.BlockSpec((X, Y), whole2),
            pl.BlockSpec((X, Y), whole2),
            pl.BlockSpec((X, Y), whole2),
            smem,
            smem,
        ],
        out_specs=pl.BlockSpec((step_m, F, X, Y), lambda i: (i, 0, 0, 0)),
        out_shape=jax.ShapeDtypeStruct((M, F, X, Y), F32),
        scratch_shapes=[
            pltpu.VMEM((2 * FX, FX), BF16),
            pltpu.VMEM((2 * FX, FX), BF16),
            pltpu.VMEM((FX, Y), F32),
        ],
        cost_estimate=pl.CostEstimate(
            flops=8 * 10**9, bytes_accessed=7 * 10**6, transcendentals=0
        ),
        name="inside",
    )(v, along, across, coll, mask, types, rates, table)


def diagonal(big, small, left, right):
    rows, cols = left * X, right * X
    own = iota((rows, cols), 0) % X == iota((rows, cols), 1) % X
    pick = (iota((cols, 128), 0) // X == iota((cols, 128), 1)).astype(F32)
    big = exact_dot(where0(own, big), pick)
    small = exact_dot(where0(own, small), pick)
    big, small = big.reshape(left, X, 128), small.reshape(left, X, 128)
    for shift in (4, 2, 1):
        big, err = two_sum(big, roll(big, shift, 1))
        small = small + roll(small, shift, 1) + err
    sel = (iota((left, rows), 1) == X * iota((left, rows), 0)).astype(F32)
    return exact_dot(sel, big.reshape(rows, 128)), exact_dot(sel, small.reshape(rows, 128))


def basis_kernel(p_ref, out_ref, acc, *, step_f):
    @pl.when(pl.program_id(0) == 0)
    def _():
        acc[...] = jnp.zeros_like(acc)

    def one(f, carry):
        hi, lo = split2(p_ref[:, f].reshape(KX, Y))
        both = jnp.concatenate([hi, lo], axis=0)
        acc[...] += half_dot(both, both, NT)
        return carry

    lax.fori_loop(0, step_f, one, 0)

    @pl.when(pl.program_id(0) == F // step_f - 1)
    def _():
        big = acc[0:KX, 0:KX]
        small = acc[0:KX, KX:] + acc[KX:, 0:KX] + acc[KX:, KX:]
        hi, lo = diagonal(big, small, K, K)
        lane = iota((8, 128), 1)
        for half, part in enumerate((hi, lo)):
            line = where0((lane >= 80) & (lane < 104), roll(part[0:8], 80, 1))
            line = line + where0((lane >= 104) & (lane < 120), roll(part[8:16], 96, 1))
            line = line + where0(lane >= 120, roll(part[16:24], 104, 1))
            out_ref[8 * half : 8 * half + 8, :] = line


def basis(p, step_f=13):
    return pl.pallas_call(
        functools.partial(basis_kernel, step_f=step_f),
        grid=(F // step_f,),
        in_specs=[pl.BlockSpec((K, step_f, X, Y), lambda i: (0, i, 0, 0))],
        out_specs=pl.BlockSpec((16, 128), lambda i: (0, 0)),
        out_shape=jax.ShapeDtypeStruct((16, 128), F32),
        scratch_shapes=[pltpu.VMEM((2 * KX, 2 * KX), F32)],
        cost_estimate=pl.CostEstimate(
            flops=8 * 10**9, bytes_accessed=5 * 10**6, transcendentals=0
        ),
        name="basis",
    )(p)


def halo_kernel(
    a_hbm, p_hbm, before_ref, after_ref, ybefore_ref, yafter_ref, along_ref, across_ref, gp_ref,
    out_hbm, line_ref, a, p, w_hi, w_lo, cb, ca, acc, sems,
):
    get_a = pltpu.make_async_copy(a_hbm, a, sems.at[0])
    get_p = pltpu.make_async_copy(p_hbm, p, sems.at[1])
    get_a.start()
    get_p.start()

    row, col = iota((FX, HALO), 0), iota((FX, HALO), 1)
    x, f = row % X, row // X
    g, j = col % (2 * F) // 2, col % 2
    left = (iota((FX, F), 0) // X == iota((FX, F), 1)).astype(F32)
    gcol = iota((F, HALO), 1) % (2 * F) // 2
    right = (gcol == iota((F, HALO), 0)).astype(F32)
    fa = 0.5 * exact_dot(exact_dot(left, along_ref[...]), right)
    same = f == g
    edge = (x == 0) & (j == 1)
    wb = where0(edge, -fa) + jnp.where(same & edge, -4.0 * DAMP, 0.0)
    wb = wb + jnp.where(same & (x == j), DAMP, 0.0)
    edge = (x == X - 1) & (j == 0)
    wa = where0(edge, fa) + jnp.where(same & edge, -4.0 * DAMP, 0.0)
    wa = wa + jnp.where(same & (x == X - 2 + j), DAMP, 0.0)
    w = jnp.concatenate([wb, wa], axis=1)
    owner = iota((FX, 2 * HALO), 1) % HALO // (2 * F)
    for i in range(2):
        hi, lo = split2(where0(owner == i, w))
        w_hi[i * FX : (i + 1) * FX, :] = hi
        w_lo[i * FX : (i + 1) * FX, :] = lo

    full = iota((FX, FX), 1) % X == iota((FX, FX), 0) % X
    wy = where0(full, 0.5 * spread(across_ref[...], FX, FX))
    lane = iota((FX, 128), 1)
    yb, ya = ybefore_ref[...], yafter_ref[...]
    term = exact_dot(wy, yb) + 4.0 * DAMP * yb
    cb[...] = DAMP * yb - where0(lane % 2 == 0, roll(term, -1, 1))
    term = exact_dot(wy, ya) - 4.0 * DAMP * ya
    ca[...] = DAMP * ya + where0(lane % 2 == 1, roll(term, 1, 1))

    get_a.wait()

    def pair(q, carry):
        h = jnp.concatenate([before_ref[q], after_ref[q]], axis=0)
        hi, lo = split2(h)
        both = half_dot(w_hi[...], hi) + half_dot(w_lo[...], hi) + half_dot(w_hi[...], lo)
        for i in range(2):
            m = 2 * q + i
            left = where0(lane < 2, roll(cb[...], (128 - 2 * m) % 128, 1))
            right = where0(lane >= 126, roll(ca[...], 126 - 2 * m, 1))
            part = a[m].reshape(FX, Y) + both[i * FX : (i + 1) * FX]
            part = part + jnp.concatenate([left, right], axis=1)
            a[m] = part.reshape(F, X, Y)
        return carry

    lax.fori_loop(0, PAIRS, pair, 0)
    put = pltpu.make_async_copy(a, out_hbm, sems.at[2])
    put.start()
    get_p.wait()
    acc[...] = jnp.zeros_like(acc)

    def field(f, carry):
        a_hi, a_lo = split2(a[:, f].reshape(MX, Y))
        p_hi, p_lo = split2(p[:, f].reshape(KX, Y))
        rows = jnp.concatenate([p_hi, a_hi, p_lo, a_lo], axis=0)
        cols = jnp.concatenate([a_hi, a_lo], axis=0)
        acc[...] += half_dot(rows, cols, NT)
        return carry

    lax.fori_loop(0, F, field, 0)
    n = KX + MX
    big = acc[0:n, 0:MX]
    small = acc[0:n, MX:] + acc[n:, 0:MX] + acc[n:, MX:]
    hi, lo = diagonal(big, small, K + M, M)
    lane = iota((8, 128), 1)
    for half, part in enumerate((hi, lo)):
        line = gp_ref[8 * half : 8 * half + 8, :]
        for i in range((K + M) // 8):
            mine = (lane >= 16 * i) & (lane < 16 * i + 16)
            line = line + where0(mine, roll(part[8 * i : 8 * i + 8], 16 * i, 1))
        for copy in range(line_ref.shape[0]):
            line_ref[copy, 8 * half : 8 * half + 8, :] = line
    put.wait()


def with_halo(a, p, before, after, ybefore, yafter, along, across, gp, copies):
    vmem = pl.BlockSpec(memory_space=pltpu.VMEM)
    anywhere = pl.BlockSpec(memory_space=pl.ANY)
    return pl.pallas_call(
        halo_kernel,
        in_specs=[anywhere, anywhere] + [vmem] * 7,
        out_specs=[anywhere, vmem],
        out_shape=[
            jax.ShapeDtypeStruct((M, F, X, Y), F32),
            jax.ShapeDtypeStruct((copies, 16, 128), F32),
        ],
        scratch_shapes=[
            pltpu.VMEM((M, F, X, Y), F32),
            pltpu.VMEM((K, F, X, Y), F32),
            pltpu.VMEM((2 * FX, 2 * HALO), BF16),
            pltpu.VMEM((2 * FX, 2 * HALO), BF16),
            pltpu.VMEM((FX, 128), F32),
            pltpu.VMEM((FX, 128), F32),
            pltpu.VMEM((2 * (KX + MX), 2 * MX), F32),
            pltpu.SemaphoreType.DMA((3,)),
        ],
        cost_estimate=pl.CostEstimate(
            flops=8 * 10**9, bytes_accessed=14 * 10**6, transcendentals=0
        ),
        name="halo",
    )(a, p, before, after, ybefore, yafter, along, across, gp)


def pair_total(ref):
    hi, lo = ref[0, 0:8, :], ref[0, 8:16, :]
    for i in range(1, ref.shape[0]):
        hi, err = two_sum(hi, ref[i, 0:8, :])
        lo = lo + ref[i, 8:16, :] + err
    return hi, lo


def middle_kernel(in_ref, out_ref):
    hi, lo = pair_total(in_ref)
    hi, lo = two_sum(hi, lo)
    for i in range(out_ref.shape[0]):
        out_ref[i, 0:8, :] = hi
        out_ref[i, 8:16, :] = lo


def middle(lines, copies):
    return pl.pallas_call(
        middle_kernel,
        out_shape=jax.ShapeDtypeStruct((copies, 16, 128), F32),
        name="middle",
    )(lines)


def sent_to_all(copies, axis):
    return lax.all_to_all(copies, axis, split_axis=0, concat_axis=0, tiled=True)


def grid_of(v, top):
    return (v + top) - top


def slices(hi, lo, axis):
    top = jnp.max(jnp.abs(hi), axis=axis, keepdims=True)
    first = grid_of(hi, top * 2.0**16)
    rest = hi - first
    second = grid_of(rest, top * 2.0**8)
    return first, second, (rest - second) + lo


def pair_dot(a, b, dims):
    a1, a2, a3 = slices(*a, dims[0][0][0])
    b1, b2, b3 = slices(*b, dims[0][1][0])
    dot = functools.partial(exact_dot, dims=dims)
    big = dot(a1, b1)
    mid = dot(a1, b2) + dot(a2, b1)
    low = dot(a1, b3) + dot(a2, b2 + b3) + dot(a3, b1 + b2)
    big, err = two_sum(big, mid)
    return two_sum(big, err + low)


def pair_add(a, b):
    big, err = two_sum(a[0], b[0])
    return two_sum(big, err + (a[1] + b[1]))


def factor(gram):
    n = gram.shape[0]
    row, lane = iota((n, 128), 0), iota((n, 128), 1)
    eye = (iota((n, n), 0) == iota((n, n), 1)).astype(F32)
    t = jnp.concatenate([gram, eye, jnp.zeros((n, 128 - 2 * n), F32)], axis=1)
    pivots = jnp.zeros((n, 128), F32)
    for k in range(n):
        column = jnp.broadcast_to(t[:, k : k + 1], (n, 128))
        pivot = jnp.broadcast_to(column[k : k + 1, :], (n, 128))
        line = jnp.broadcast_to(t[k : k + 1, :], (n, 128))
        pivots = jnp.where(row == k, pivot, pivots)
        t = t - where0(row > k, column / pivot) * line
    t = t / jnp.sqrt(pivots)
    upper = where0(row <= lane, t)[:, 0:n]
    return upper, t[:, n : 2 * n]


def final_kernel(
    line_ref, a_hbm, p_hbm, out_hbm, proj_ref, tri_ref,
    a, p, out, ma, mp, in_sems, out_sems, *, cells, parts,
):
    size = F // parts
    gets = []
    for i in range(parts):
        part = pl.ds(i * size, size)
        gets.append(
            (
                pltpu.make_async_copy(a_hbm.at[:, part], a.at[:, part], in_sems.at[0, i]),
                pltpu.make_async_copy(p_hbm.at[:, part], p.at[:, part], in_sems.at[1, i]),
            )
        )
        for get in gets[-1]:
            get.start()

    hi, lo = pair_total(line_ref)
    hi, lo = two_sum(hi, lo)
    odd = cells
    while odd % 2 == 0:
        odd //= 2
    scale = float(odd) / float(cells)
    guess = hi / float(odd)
    big = guess * 4097.0
    big = big - (big - guess)
    left = ((hi - big * float(odd)) - (guess - big) * float(odd)) + lo
    hi, lo = two_sum(guess, left / float(odd))
    hi, lo = hi * scale, lo * scale

    lane8 = iota((8, 128), 1)

    def unpack(v):
        rows = [roll(v, -16 * i, 1) for i in range(5)]
        top = where0(lane8 < 24, roll(v, -80, 1))
        centre = where0((lane8 >= 8) & (lane8 < 24), roll(v, -96, 1))
        end = where0((lane8 >= 16) & (lane8 < 24), roll(v, -104, 1))
        upper = jnp.concatenate([top, centre, end], axis=0)[:, 0:K]
        off = where0(iota((K, K), 1) // 8 > iota((K, K), 0) // 8, upper)
        eye = (iota((K, K), 0) == iota((K, K), 1)).astype(F32)
        return (
            jnp.concatenate(rows[0:3], axis=0)[:, 0:M],
            jnp.concatenate(rows[3:5], axis=0)[:, 0:M],
            upper + exact_dot(eye, off, NT),
        )

    (c_hi, s_hi, g_hi), (c_lo, s_lo, g_lo) = unpack(hi), unpack(lo)
    zero = jnp.zeros((K, M), F32)
    second = c_hi - exact_dot(g_hi, c_hi)
    proj = c_hi + second
    proj_ref[...] = proj
    gp = pair_dot((g_hi, g_lo), (proj, zero), NN)
    t_hi, t_lo = pair_add(gp, (-c_hi, -c_lo))
    gram = pair_dot(
        (jnp.concatenate([proj, c_hi], axis=0), jnp.concatenate([zero, c_lo], axis=0)),
        (jnp.concatenate([t_hi, -proj], axis=0), jnp.concatenate([t_lo, zero], axis=0)),
        TN,
    )
    gram = pair_add((s_hi, s_lo), gram)
    upper_one, inv_one = factor(gram[0])
    none = jnp.zeros((M, M), F32)
    again = pair_dot((inv_one, none), gram, NN)
    again = pair_dot(again, (inv_one, none), NT)
    upper_two, inv_two = factor(again[0] + again[1])
    tri_ref[...] = exact_dot(upper_two, upper_one)
    mix = exact_dot(inv_two, inv_one)
    mix_p = -exact_dot(mix, proj, NT)

    row, col = iota((MX, MX), 0), iota((MX, MX), 1)
    m1, m2, m3 = split3(where0(row % X == col % X, spread(mix, MX, MX)))
    ma[0] = jnp.concatenate([m1, m1], axis=1)
    ma[1] = jnp.concatenate([m2, m2], axis=1)
    ma[2] = jnp.concatenate([m3, jnp.zeros_like(m3)], axis=1)
    row, col = iota((MX, KX), 0), iota((MX, KX), 1)
    n1, n2 = split2(where0(row % X == col % X, spread(mix_p, MX, KX)))
    mp[0] = n1
    mp[1] = n2

    def field(f, carry):
        a1, a2, a3 = split3(a[:, f].reshape(MX, Y))
        p1, p2 = split2(p[:, f].reshape(KX, Y))
        both = jnp.concatenate([a1, a2], axis=0)
        total = half_dot(mp[0], p2) + half_dot(mp[1], p1) + half_dot(ma[2], both)
        total = total + half_dot(ma[0][:, 0:MX], a3) + half_dot(ma[1], both)
        total = total + half_dot(mp[0], p1) + half_dot(ma[0], both)
        out[:, f] = total.reshape(M, X, Y)
        return carry

    puts = []
    for i in range(parts):
        for get in gets[i]:
            get.wait()
        lax.fori_loop(i * size, (i + 1) * size, field, 0)
        part = pl.ds(i * size, size)
        puts.append(pltpu.make_async_copy(out.at[:, part], out_hbm.at[:, part], out_sems.at[i]))
        puts[-1].start()
    for put in puts:
        put.wait()


def final(lines, a, p, cells, parts=2):
    vmem = pl.BlockSpec(memory_space=pltpu.VMEM)
    anywhere = pl.BlockSpec(memory_space=pl.ANY)
    return pl.pallas_call(
        functools.partial(final_kernel, cells=cells, parts=parts),
        in_specs=[vmem, anywhere, anywhere],
        out_specs=[anywhere, vmem, vmem],
        out_shape=[
            jax.ShapeDtypeStruct((M, F, X, Y), F32),
            jax.ShapeDtypeStruct((K, M), F32),
            jax.ShapeDtypeStruct((M, M), F32),
        ],
        scratch_shapes=[
            pltpu.VMEM((M, F, X, Y), F32),
            pltpu.VMEM((K, F, X, Y), F32),
            pltpu.VMEM((M, F, X, Y), F32),
            pltpu.VMEM((3, MX, 2 * MX), BF16),
            pltpu.VMEM((2, MX, KX), BF16),
            pltpu.SemaphoreType.DMA((2, parts)),
            pltpu.SemaphoreType.DMA((parts,)),
        ],
        name="final",
    )(lines, a, p)


def on_device(
    krylov_block, prior_basis, flux_along, flux_across, collision, field_rates, wall_table,
    wall_mask, wall_type,
):
    cells = F * X * lax.axis_size(GX) * Y * lax.axis_size(GY)
    first, last, yfirst, ylast = pack(krylov_block)

    def onward(axis):
        return [(i, i + 1) for i in range(lax.axis_size(axis) - 1)]

    def back(axis):
        return [(j, i) for i, j in onward(axis)]

    before = lax.ppermute(last, GX, onward(GX))
    after = lax.ppermute(first, GX, back(GX))
    ybefore = lax.ppermute(ylast, GY, onward(GY))
    yafter = lax.ppermute(yfirst, GY, back(GY))
    applied = inside(
        krylov_block, flux_along, flux_across, collision, wall_mask, wall_type, field_rates,
        wall_table,
    )
    gp = basis(prior_basis)
    sizes = [lax.axis_size(stage) for stage in STAGES]
    applied, lines = with_halo(
        applied, prior_basis, before, after, ybefore, yafter, flux_along, flux_across, gp, sizes[0]
    )
    lines = middle(sent_to_all(lines, STAGES[0]), sizes[1])
    lines = sent_to_all(lines, STAGES[1])
    return final(lines, applied, prior_basis, cells)


def solution(mesh):
    torus = Mesh(mesh.devices.reshape(8, 4, 4, 2), ("gx_z", "gx_x", "gy_y", "gy_c"))
    cells = P(GX, GY)
    stack = P(None, None, GX, GY)
    in_specs = (stack, stack, P(), P(), cells, P(), P(), cells, cells)
    out_specs = (stack, P(), P())
    return jax.shard_map(
        on_device, mesh=torus, in_specs=in_specs, out_specs=out_specs, check_vma=False
    )
```

profile of v0, /device:TPU:1, one launch (start us, length us, event | category | flops | bytes accessed | tf_op | source)
XLA Modules:
  0.0 111.7 jit_solution(14019846507758520319)
XLA Ops:
  0.6 4.7 %pack.1 = (f32[8,104,256]{2,1,0:T(8,128)}, f32[8,104,256]{2,1,0:T(8,128)}, f32[208,128]{1,0:T(8,128)}, f32[208,128]{1,0:T(8,128)}) custom-call(f32[16,26,8,256]{3,2,1,0:T(8,128)} %v_ref.3), custom_call_target="tpu_custom_call" | custom-call | flops 1000000 | bytes 6000000 | tf_op jit(solution)/shard_map/pack/pallas_call | solution.py:104
  5.3 4.6 %collective-permute-start.2 = (f32[208,128]{1,0:T(8,128)}, f32[208,128]{1,0:T(8,128)S(1)}, u32[]{:S(2)}, u32[]{:S(2)}) collective-permute-start(f32[208,128]{1,0:T(8,128)} %get-tuple-element.11), channel_id=1, source_target_pairs={{0,1},{1,2},{2,3},{3,4},{4,5},{5,6},{6,7},{8,9},{9,10},{10,11},{11... | collective-permute-start | bytes 319496 | tf_op jit(solution)/shard_map/ppermute | solution.py:586
  9.9 1.9 %collective-permute-start.3 = (f32[208,128]{1,0:T(8,128)}, f32[208,128]{1,0:T(8,128)S(1)}, u32[]{:S(2)}, u32[]{:S(2)}) collective-permute-start(f32[208,128]{1,0:T(8,128)} %get-tuple-element.12), channel_id=1, source_target_pairs={{1,0},{2,1},{3,2},{4,3},{5,4},{6,5},{7,6},{9,8},{10,9},{11,10},{12... | collective-permute-start | bytes 319496 | tf_op jit(solution)/shard_map/ppermute | solution.py:587
  11.8 3.2 %collective-permute-start = (f32[8,104,256]{2,1,0:T(8,128)}, f32[8,104,256]{2,1,0:T(8,128)S(1)}, u32[]{:S(2)}, u32[]{:S(2)}) collective-permute-start(f32[8,104,256]{2,1,0:T(8,128)} %get-tuple-element.9), channel_id=1, source_target_pairs={{0,8},{8,16},{16,24},{24,32},{32,40},{40,48},{48,56},{56,64},{64,7... | collective-permute-start | bytes 2555912 | tf_op jit(solution)/shard_map/ppermute | solution.py:584
  15.0 1.3 %collective-permute-start.1 = (f32[8,104,256]{2,1,0:T(8,128)}, f32[8,104,256]{2,1,0:T(8,128)S(1)}, u32[]{:S(2)}, u32[]{:S(2)}) collective-permute-start(f32[8,104,256]{2,1,0:T(8,128)} %get-tuple-element.10), channel_id=1, source_target_pairs={{8,0},{16,8},{24,16},{32,24},{40,32},{48,40},{56,48},{64,56},{72,6... | collective-permute-start | bytes 2555912 | tf_op jit(solution)/shard_map/ppermute | solution.py:585
  16.3 10.8 %basis.1.gp_ref = f32[16,128]{1,0:T(8,128)} custom-call(f32[24,26,8,256]{3,2,1,0:T(8,128)} %p_hbm.3), custom_call_target="tpu_custom_call" | custom-call | flops 8000000000 | bytes 5000000 | tf_op jit(solution)/shard_map/basis/pallas_call | solution.py:247
  27.1 10.7 %inside.1.a_hbm = f32[16,26,8,256]{3,2,1,0:T(8,128)} custom-call(f32[16,26,8,256]{3,2,1,0:T(8,128)} %v_ref.3, f32[26,26]{1,0:T(8,128)} %along_ref.3, f32[26,26]{1,0:T(8,128)} %across_ref.3, f32[8,256]{1,0:T(8,128)} %coll_ref.1, s32[8,256]{1,0:T(8,128)} %mask_ref.1, s32[8,256]{1,0:T(8,128)} %type_ref.1, f32[26]{0:T(128)} %rate_ref.1, f32[4,26]{1,0:T(4,128)} %table_ref.1), custom_call_target="tpu_custom_call" | custom-call | flops 8000000000 | bytes 7000000 | tf_op jit(solution)/shard_map/inside/pallas_call | solution.py:179
  37.8 0.0 collective-permute-done.2.ybefore_ref
  37.8 0.0 copy-start.2
  37.8 0.0 collective-permute-done.3.yafter_ref
  37.8 0.0 copy-start.3
  37.8 0.0 collective-permute-done.before_ref
  37.9 0.0 copy-start
  37.9 0.0 collective-permute-done.1.after_ref
  37.9 0.6 copy-done.2
  38.5 0.1 copy-done.3
  38.5 0.3 copy-done
  38.9 0.9 copy-done.1
  39.8 15.3 %halo.1 = (f32[16,26,8,256]{3,2,1,0:T(8,128)}, f32[16,16,128]{2,1,0:T(8,128)}) custom-call(f32[16,26,8,256]{3,2,1,0:T(8,128)} %inside.1.a_hbm, f32[24,26,8,256]{3,2,1,0:T(8,128)} %p_hbm.3, f32[8,104,256]{2,1,0:T(8,128)} %copy-done, f32[8,104,256]{2,1,0:T(8,128)} %copy-done.1, f32[208,128]{1,0:T(8,128)} %copy-done.2, f32[208,128]{1,0:T(8,128)} %copy-done.3, ...), custom_call_target="tpu_custom_call" | custom-call | flops 8000000000 | bytes 14000000 | tf_op jit(solution)/shard_map/halo/pallas_call | solution.py:348
  55.1 14.1 %all_to_all.10.in_ref = f32[16,16,128]{2,1,0:T(8,128)} all-to-all(f32[16,16,128]{2,1,0:T(8,128)} %get-tuple-element.13), channel_id=1, replica_groups=mesh['gx_z'=8,'gx_x'=4,'gy_y'=4,'gy_c'=2] {'gx_x','gy_y'}, dimensions={0} | all-to-all | bytes 262144 | tf_op jit(solution)/shard_map/all_to_all | solution.py:398
  69.2 1.6 %middle.1 = f32[16,16,128]{2,1,0:T(8,128)} custom-call(f32[16,16,128]{2,1,0:T(8,128)} %all_to_all.10.in_ref), custom_call_target="tpu_custom_call" | custom-call | tf_op jit(solution)/shard_map/middle/pallas_call | solution.py:390
  70.8 21.1 %all_to_all.11.line_ref = f32[16,16,128]{2,1,0:T(8,128)} all-to-all(f32[16,16,128]{2,1,0:T(8,128)} %middle.1), channel_id=1, replica_groups=mesh['gx_z'=8,'gx_x'=4,'gy_y'=4,'gy_c'=2] {'gx_z','gy_c'}, dimensions={0} | all-to-all | bytes 262144 | tf_op jit(solution)/shard_map/all_to_all | solution.py:398
  91.9 18.3 %final.1 = (f32[16,26,8,256]{3,2,1,0:T(8,128)}, f32[24,16]{1,0:T(8,128)}, f32[16,16]{1,0:T(8,128)}) custom-call(f32[16,16,128]{2,1,0:T(8,128)} %all_to_all.11.line_ref, f32[16,26,8,256]{3,2,1,0:T(8,128)} %get-tuple-element.14.a_hbm, f32[24,26,8,256]{3,2,1,0:T(8,128)} %p_hbm.3), custom_call_target="tpu_custom_call" | custom-call | tf_op jit(solution)/shard_map/final/pallas_call | solution.py:549
  110.3 1.4 %copy.12 = f32[24,16]{0,1:T(8,128)} copy(f32[24,16]{1,0:T(8,128)} %get-tuple-element.16) | data formatting | bytes 3072 | tf_op jit(solution)/shard_map/final/pallas_call | solution.py:549
  (1 shorter events, 0.0 us)
Async XLA Ops:
  5.3 32.5 %collective-permute-start.2 = (f32[208,128]{1,0:T(8,128)}, f32[208,128]{1,0:T(8,128)S(1)}, u32[]{:S(2)}, u32[]{:S(2)}) collective-permute-start(f32[208,128]{1,0:T(8,128)} %get-tuple-element.11), channel_id=1, source_target_pairs={{0,1},{1,2},{2,3},{3,4},{4,5},{5,6},{6,7},{8,9},{9,10},{10,11},{11... | collective-permute-start | bytes 319496 | tf_op jit(solution)/shard_map/ppermute | solution.py:586
  9.9 28.0 %collective-permute-start.3 = (f32[208,128]{1,0:T(8,128)}, f32[208,128]{1,0:T(8,128)S(1)}, u32[]{:S(2)}, u32[]{:S(2)}) collective-permute-start(f32[208,128]{1,0:T(8,128)} %get-tuple-element.12), channel_id=1, source_target_pairs={{1,0},{2,1},{3,2},{4,3},{5,4},{6,5},{7,6},{9,8},{10,9},{11,10},{12... | collective-permute-start | bytes 319496 | tf_op jit(solution)/shard_map/ppermute | solution.py:587
  11.8 26.1 %collective-permute-start = (f32[8,104,256]{2,1,0:T(8,128)}, f32[8,104,256]{2,1,0:T(8,128)S(1)}, u32[]{:S(2)}, u32[]{:S(2)}) collective-permute-start(f32[8,104,256]{2,1,0:T(8,128)} %get-tuple-element.9), channel_id=1, source_target_pairs={{0,8},{8,16},{16,24},{24,32},{32,40},{40,48},{48,56},{56,64},{64,7... | collective-permute-start | bytes 2555912 | tf_op jit(solution)/shard_map/ppermute | solution.py:584
  15.0 22.9 %collective-permute-start.1 = (f32[8,104,256]{2,1,0:T(8,128)}, f32[8,104,256]{2,1,0:T(8,128)S(1)}, u32[]{:S(2)}, u32[]{:S(2)}) collective-permute-start(f32[8,104,256]{2,1,0:T(8,128)} %get-tuple-element.10), channel_id=1, source_target_pairs={{8,0},{16,8},{24,16},{32,24},{40,32},{48,40},{56,48},{64,56},{72,6... | collective-permute-start | bytes 2555912 | tf_op jit(solution)/shard_map/ppermute | solution.py:585
  37.8 0.6 copy-start.2
  37.8 0.7 copy-start.3
  37.9 1.0 copy-start
  38.9 0.9 copy-start.1
where the time goes:
time: 112 us
  Pallas kernels  61.4 us (55%)
  blocking collectives  35.2 us (31%)
  starting transfers between devices  11 us (10%)
  local copies, waits for them, and re-layouts  3.29 us (3%)
    all_to_all x2, blocking collectives, sent_to_all(): return lax.all_to_all(copies, axis, split_axis=0, concat_axis=0, tiled=True)  35.2 us
    pallas_call x1, Pallas kernels, final(): pl.pallas_call(functools.partial(final_kernel, cells=cells, parts=parts),...  18.3 us
    pallas_call x1, Pallas kernels, with_halo(): pl.pallas_call(halo_kernel, in_specs=[anywhere, anywhere] + [vmem] * 7, o...  15.3 us
    pallas_call x1, Pallas kernels, basis(): pl.pallas_call(functools.partial(basis_kernel, step_f=step_f), grid=(F //...  10.8 us
    pallas_call x1, Pallas kernels, inside(): pl.pallas_call(functools.partial(inside_kernel, step_m=step_m), grid=(M /...  10.7 us
    pallas_call x1, Pallas kernels, pack(): pl.pallas_call(functools.partial(pack_kernel, step_m=step_m), grid=(M //...  4.66 us
    ppermute x1, starting transfers between devices, on_device(): ybefore = lax.ppermute(ylast, GY, onward(GY))  4.57 us
    ppermute x1, starting transfers between devices, on_device(): before = lax.ppermute(last, GX, onward(GX))  3.17 us
  transfers between devices with their start and end apart: 4, of which 0 were waited for; matrix products, arithmetic and copies ran while one was open for 0% of the time, Pallas kernels for 19%

commit v1 on v0

v1 whole, which is shorter than its diff:
```python
import functools

import jax
import jax.numpy as jnp
from jax import lax
from jax.experimental import pallas as pl
from jax.experimental.pallas import tpu as pltpu
from jax.sharding import Mesh
from jax.sharding import PartitionSpec as P

GX = ("gx_z", "gx_x")
GY = ("gy_y", "gy_c")
STAGES = (("gx_x", "gy_y"), ("gx_z", "gy_c"))

DAMP = 0.0625
PRECISE = lax.Precision.HIGHEST
F32 = jnp.float32
BF16 = jnp.bfloat16

M = 16
K = 24
F = 26
X = 8
Y = 256
FX = F * X
MX = M * X
KX = K * X
PAIRS = M // 2
HALO = 4 * F

NN = (((1,), (0,)), ((), ()))
NT = (((1,), (1,)), ((), ()))
TN = (((0,), (0,)), ((), ()))


def exact_dot(a, b, dims=NN):
    return lax.dot_general(a, b, dims, precision=PRECISE, preferred_element_type=F32)


def half_dot(a, b, dims=NN):
    return lax.dot_general(a, b, dims, preferred_element_type=F32)


def split2(v):
    hi = v.astype(BF16)
    return hi, (v - hi.astype(F32)).astype(BF16)


def split3(v):
    hi = v.astype(BF16)
    rest = v - hi.astype(F32)
    mid = rest.astype(BF16)
    return hi, mid, (rest - mid.astype(F32)).astype(BF16)


def iota(shape, dim):
    return lax.broadcasted_iota(jnp.int32, shape, dim)


def where0(mask, v):
    return jnp.where(mask, v, jnp.zeros_like(v))


def spread(small, rows, cols):
    n, k = small.shape
    left = (iota((rows, n), 0) // X == iota((rows, n), 1)).astype(F32)
    right = (iota((k, cols), 1) // X == iota((k, cols), 0)).astype(F32)
    return exact_dot(exact_dot(left, small), right)


def two_sum(a, b):
    s = a + b
    t = s - a
    return s, (a - (s - t)) + (b - t)


def roll(v, shift, axis):
    size = v.shape[axis]
    return pltpu.roll(v, shift % size if isinstance(shift, int) else shift, axis)


def pack_kernel(v_ref, first_ref, last_ref, *, step_m):
    for i in range(step_m):
        for f in range(F):
            at = (i % 2 * F + f) * 2
            first_ref[i // 2, at : at + 2, :] = v_ref[i, f, 0:2, :]
            last_ref[i // 2, at : at + 2, :] = v_ref[i, f, X - 2 : X, :]


def pack(v, step_m=4):
    return pl.pallas_call(
        functools.partial(pack_kernel, step_m=step_m),
        grid=(M // step_m,),
        in_specs=[pl.BlockSpec((step_m, F, X, Y), lambda i: (i, 0, 0, 0))],
        out_specs=[pl.BlockSpec((step_m // 2, HALO, Y), lambda i: (i, 0, 0))] * 2,
        out_shape=[jax.ShapeDtypeStruct((PAIRS, HALO, Y), F32)] * 2,
        cost_estimate=pl.CostEstimate(flops=10**6, bytes_accessed=6 * 10**6, transcendentals=0),
        name="pack",
    )(v)


def inside_kernel(
    v_ref, along_ref, across_ref, coll_ref, mask_ref, type_ref, rate_ref, table_ref,
    out_ref, yfirst_ref, ylast_ref, halo_ref, w, coeff, *, step_m,
):
    @pl.when(pl.program_id(0) == 0)
    def _():
        row, col = iota((FX, FX), 0), iota((FX, FX), 1)
        same_f = row // X == col // X
        step = col % X - row % X
        fa = spread(along_ref[...], FX, FX)
        fc = spread(across_ref[...], FX, FX)
        wx = where0(step == 1, 0.5 * fa) - where0(step == -1, 0.5 * fa)
        near = same_f & (jnp.abs(step) == 1)
        far = same_f & (jnp.abs(step) == 2)
        wx = wx + jnp.where(near, -4.0 * DAMP, 0.0) + jnp.where(far, DAMP, 0.0)
        wy = where0(step == 0, 0.5 * fc)
        for i, part in enumerate((wx, wy)):
            hi, lo = split2(part)
            w[0, i * FX : (i + 1) * FX, :] = hi
            w[1, i * FX : (i + 1) * FX, :] = lo
        walls = [
            jnp.where(type_ref[...] == t, mask_ref[...].astype(F32), 0.0)
            for t in range(table_ref.shape[0])
        ]
        for f in range(F):
            c = coll_ref[...] * rate_ref[f]
            for t, wall in enumerate(walls):
                c = c + wall * table_ref[t, f]
            coeff[f * X : (f + 1) * X, :] = c + 12.0 * DAMP

        row, col = iota((FX, HALO), 0), iota((FX, HALO), 1)
        x, f = row % X, row // X
        g, j, later = col % (2 * F) // 2, col % 2, col >= 2 * F
        left = (iota((FX, F), 0) // X == iota((FX, F), 1)).astype(F32)
        right = (iota((F, HALO), 1) % (2 * F) // 2 == iota((F, HALO), 0)).astype(F32)
        fa = 0.5 * exact_dot(exact_dot(left, along_ref[...]), right)
        same = f == g
        edge_b = (x == 0) & (j == 1) & ~later
        edge_a = (x == X - 1) & (j == 0) & later
        wh = where0(edge_a, fa) - where0(edge_b, fa)
        wh = wh + jnp.where(same & (edge_a | edge_b), -4.0 * DAMP, 0.0)
        outer = ((x == j) & ~later) | ((x == X - 2 + j) & later)
        wh = wh + jnp.where(same & outer, DAMP, 0.0)
        hi = wh.astype(BF16).astype(F32)
        halo_ref[0] = jnp.concatenate([hi, hi], axis=1).astype(BF16)
        halo_ref[1] = jnp.concatenate([wh - hi, jnp.zeros_like(wh)], axis=1).astype(BF16)
        yfirst_ref[...] = jnp.zeros_like(yfirst_ref)
        ylast_ref[...] = jnp.zeros_like(ylast_ref)

    lane = iota((FX, Y), 1)
    lane2 = iota((FX, 128), 1) // 2

    def one(i, carry):
        m = pl.program_id(0) * step_m + i
        v = v_ref[i].reshape(FX, Y)
        mine = lane2 == m
        yfirst_ref[...] = jnp.where(mine, roll(v[:, 0:128], 2 * m, 1), yfirst_ref[...])
        ylast_ref[...] = jnp.where(mine, roll(v[:, Y - 128 :], 2 * m + 2, 1), ylast_ref[...])
        hi, lo = split2(v)
        left = jnp.concatenate([w[0], w[1], w[0]], axis=1)
        both = half_dot(left, jnp.concatenate([hi, hi, lo], axis=0))
        u = both[FX:]
        out = both[:FX] + coeff[...] * v
        side = 4.0 * DAMP * v
        out = out + where0(lane < Y - 1, roll(u - side, -1, 1))
        out = out - where0(lane > 0, roll(u + side, 1, 1))
        two = DAMP * v
        out = out + where0(lane < Y - 2, roll(two, -2, 1)) + where0(lane > 1, roll(two, 2, 1))
        out_ref[i] = out.reshape(F, X, Y)
        return carry

    lax.fori_loop(0, step_m, one, 0)


def inside(v, along, across, coll, mask, types, rates, table, step_m=4):
    smem = pl.BlockSpec(memory_space=pltpu.SMEM)
    whole2 = lambda i: (0, 0)
    return pl.pallas_call(
        functools.partial(inside_kernel, step_m=step_m),
        grid=(M // step_m,),
        in_specs=[
            pl.BlockSpec((step_m, F, X, Y), lambda i: (i, 0, 0, 0)),
            pl.BlockSpec((F, F), whole2),
            pl.BlockSpec((F, F), whole2),
            pl.BlockSpec((X, Y), whole2),
            pl.BlockSpec((X, Y), whole2),
            pl.BlockSpec((X, Y), whole2),
            smem,
            smem,
        ],
        out_specs=[
            pl.BlockSpec((step_m, F, X, Y), lambda i: (i, 0, 0, 0)),
            pl.BlockSpec((FX, 128), whole2),
            pl.BlockSpec((FX, 128), whole2),
            pl.BlockSpec((2, FX, 2 * HALO), lambda i: (0, 0, 0)),
        ],
        out_shape=[
            jax.ShapeDtypeStruct((M, F, X, Y), F32),
            jax.ShapeDtypeStruct((FX, 128), F32),
            jax.ShapeDtypeStruct((FX, 128), F32),
            jax.ShapeDtypeStruct((2, FX, 2 * HALO), BF16),
        ],
        scratch_shapes=[pltpu.VMEM((2, 2 * FX, FX), BF16), pltpu.VMEM((FX, Y), F32)],
        cost_estimate=pl.CostEstimate(
            flops=8 * 10**9, bytes_accessed=7 * 10**6, transcendentals=0
        ),
        name="inside",
    )(v, along, across, coll, mask, types, rates, table)


def columns_kernel(ybefore_ref, yafter_ref, across_ref, cb_ref, ca_ref):
    full = iota((FX, FX), 1) % X == iota((FX, FX), 0) % X
    wy = where0(full, 0.5 * spread(across_ref[...], FX, FX))
    lane = iota((FX, 128), 1)
    yb, ya = ybefore_ref[...], yafter_ref[...]
    term = exact_dot(wy, yb) + 4.0 * DAMP * yb
    cb_ref[...] = DAMP * yb - where0(lane % 2 == 0, roll(term, -1, 1))
    term = exact_dot(wy, ya) - 4.0 * DAMP * ya
    ca_ref[...] = DAMP * ya + where0(lane % 2 == 1, roll(term, 1, 1))


def columns(ybefore, yafter, across):
    return pl.pallas_call(
        columns_kernel,
        out_shape=[jax.ShapeDtypeStruct((FX, 128), F32)] * 2,
        cost_estimate=pl.CostEstimate(flops=10**8, bytes_accessed=10**6, transcendentals=0),
        name="columns",
    )(ybefore, yafter, across)


def diagonal(big, small, left, right):
    rows, cols = left * X, right * X
    own = iota((rows, cols), 0) % X == iota((rows, cols), 1) % X
    pick = (iota((cols, 128), 0) // X == iota((cols, 128), 1)).astype(F32)
    big = exact_dot(where0(own, big), pick)
    small = exact_dot(where0(own, small), pick)
    big, small = big.reshape(left, X, 128), small.reshape(left, X, 128)
    for shift in (4, 2, 1):
        big, err = two_sum(big, roll(big, shift, 1))
        small = small + roll(small, shift, 1) + err
    sel = (iota((left, rows), 1) == X * iota((left, rows), 0)).astype(F32)
    return exact_dot(sel, big.reshape(rows, 128)), exact_dot(sel, small.reshape(rows, 128))


TWO = F // 2


def basis_kernel(p_hbm, out_ref, hi_hbm, lo_hbm, p, hi_ref, lo_ref, big_ref, small_ref, in_sem, out_sem):
    def get(q):
        return pltpu.make_async_copy(
            p_hbm.at[:, pl.ds(2 * q, 2)], p.at[:, pl.ds(2 * q, 2)], in_sem.at[q]
        )

    def puts(q):
        at = pl.ds(2 * q, 2)
        return (
            pltpu.make_async_copy(hi_ref.at[at], hi_hbm.at[at], out_sem.at[0, q]),
            pltpu.make_async_copy(lo_ref.at[at], lo_hbm.at[at], out_sem.at[1, q]),
        )

    for q in range(TWO):
        get(q).start()
    big_ref[...] = jnp.zeros_like(big_ref)
    small_ref[...] = jnp.zeros_like(small_ref)

    def two(q, carry):
        get(q).wait()
        his, los = [], []
        for i in range(2):
            hi, lo = split2(p[:, 2 * q + i].reshape(KX, Y))
            hi_ref[2 * q + i] = hi
            lo_ref[2 * q + i] = lo
            his.append(hi)
            los.append(lo)
        hi = jnp.concatenate(his, axis=1)
        lo = jnp.concatenate(los, axis=1)
        for put in puts(q):
            put.start()
        big_ref[...] += half_dot(hi, hi, NT)
        half = lo * jnp.asarray(0.5, BF16)
        small_ref[...] += half_dot(
            jnp.concatenate([lo, lo], axis=1), jnp.concatenate([hi, half], axis=1), NT
        )
        return carry

    lax.fori_loop(0, TWO, two, 0)
    hi, lo = diagonal(big_ref[...], small_ref[...], K, K)
    eye = (iota((K, K), 0) == iota((K, 128), 1)[:, 0:K]).astype(F32)
    turned = exact_dot(lo[:, 0:K], eye, TN)
    lo = lo + jnp.concatenate([turned, jnp.zeros((K, 128 - K), F32)], axis=1)
    lane = iota((8, 128), 1)
    for half, part in enumerate((hi, lo)):
        line = where0((lane >= 80) & (lane < 104), roll(part[0:8], 80, 1))
        line = line + where0((lane >= 104) & (lane < 120), roll(part[8:16], 96, 1))
        line = line + where0(lane >= 120, roll(part[16:24], 104, 1))
        out_ref[8 * half : 8 * half + 8, :] = line

    def end(q, carry):
        for put in puts(q):
            put.wait()
        return carry

    lax.fori_loop(0, TWO, end, 0)


def basis(p):
    anywhere = pl.BlockSpec(memory_space=pl.ANY)
    return pl.pallas_call(
        basis_kernel,
        in_specs=[anywhere],
        out_specs=[pl.BlockSpec(memory_space=pltpu.VMEM), anywhere, anywhere],
        out_shape=[
            jax.ShapeDtypeStruct((16, 128), F32),
            jax.ShapeDtypeStruct((F, KX, Y), BF16),
            jax.ShapeDtypeStruct((F, KX, Y), BF16),
        ],
        scratch_shapes=[
            pltpu.VMEM((K, F, X, Y), F32),
            pltpu.VMEM((F, KX, Y), BF16),
            pltpu.VMEM((F, KX, Y), BF16),
            pltpu.VMEM((KX, KX), F32),
            pltpu.VMEM((KX, KX), F32),
            pltpu.SemaphoreType.DMA((TWO,)),
            pltpu.SemaphoreType.DMA((2, TWO)),
        ],
        cost_estimate=pl.CostEstimate(
            flops=8 * 10**9, bytes_accessed=10 * 10**6, transcendentals=0
        ),
        name="basis",
    )(p)


def halo_kernel(
    a_hbm, hi_hbm, lo_hbm, before_hbm, after_hbm, cb_ref, ca_ref, w_ref, gp_ref,
    out_hbm, line_ref, a, p_hi, p_lo, before, after, acc, a_sem, sems,
):
    def get(q):
        at = pl.ds(2 * q, 2)
        return (
            pltpu.make_async_copy(a_hbm.at[at], a.at[at], a_sem.at[0, q]),
            pltpu.make_async_copy(before_hbm.at[q], before.at[q], a_sem.at[1, q]),
            pltpu.make_async_copy(after_hbm.at[q], after.at[q], a_sem.at[2, q]),
        )

    def put(q):
        at = pl.ds(2 * q, 2)
        return pltpu.make_async_copy(a.at[at], out_hbm.at[at], a_sem.at[3, q])

    get_hi = pltpu.make_async_copy(hi_hbm, p_hi, sems.at[0])
    get_lo = pltpu.make_async_copy(lo_hbm, p_lo, sems.at[1])
    for q in range(PAIRS):
        for each in get(q):
            each.start()
    get_hi.start()
    get_lo.start()
    lane = iota((FX, 128), 1)

    def pair(q, carry):
        for each in get(q):
            each.wait()
        for i in range(2):
            m = 2 * q + i
            mine = slice(i * 2 * F, (i + 1) * 2 * F)
            h = jnp.concatenate([before[q][mine], after[q][mine]], axis=0)
            hi = h.astype(BF16).astype(F32)
            h = jnp.concatenate([hi, h - hi], axis=0).astype(BF16)
            left = where0(lane < 2, roll(cb_ref[...], (128 - 2 * m) % 128, 1))
            right = where0(lane >= 126, roll(ca_ref[...], 126 - 2 * m, 1))
            part = a[m].reshape(FX, Y) + jnp.concatenate([left, right], axis=1)
            part = part + (half_dot(w_ref[0], h) + half_dot(w_ref[1], h))
            a[m] = part.reshape(F, X, Y)
        put(q).start()
        return carry

    lax.fori_loop(0, PAIRS, pair, 0)
    acc[...] = jnp.zeros_like(acc)
    get_hi.wait()
    get_lo.wait()

    def two(q, carry):
        his, los, p_his, p_los = [], [], [], []
        for i in range(2):
            hi, lo = split2(a[:, 2 * q + i].reshape(MX, Y))
            his.append(hi)
            los.append(lo)
            p_his.append(p_hi[2 * q + i])
            p_los.append(p_lo[2 * q + i])
        hi, lo, ph, pl_ = (jnp.concatenate(v, axis=1) for v in (his, los, p_his, p_los))
        rows = jnp.concatenate([ph, hi, pl_, lo], axis=0)
        acc[...] += half_dot(rows, jnp.concatenate([hi, lo], axis=0), NT)
        return carry

    lax.fori_loop(0, TWO, two, 0)
    n = KX + MX
    big = acc[0:n, 0:MX]
    small = acc[0:n, MX:] + acc[n:, 0:MX] + acc[n:, MX:]
    hi, lo = diagonal(big, small, K + M, M)
    lane = iota((8, 128), 1)
    for half, part in enumerate((hi, lo)):
        line = gp_ref[8 * half : 8 * half + 8, :]
        for i in range((K + M) // 8):
            mine = (lane >= 16 * i) & (lane < 16 * i + 16)
            line = line + where0(mine, roll(part[8 * i : 8 * i + 8], 16 * i, 1))
        for copy in range(line_ref.shape[0]):
            line_ref[copy, 8 * half : 8 * half + 8, :] = line

    def end(q, carry):
        put(q).wait()
        return carry

    lax.fori_loop(0, PAIRS, end, 0)


def with_halo(a, p_hi, p_lo, before, after, cb, ca, weights, gp, copies):
    vmem = pl.BlockSpec(memory_space=pltpu.VMEM)
    anywhere = pl.BlockSpec(memory_space=pl.ANY)
    return pl.pallas_call(
        halo_kernel,
        in_specs=[anywhere] * 5 + [vmem] * 4,
        out_specs=[anywhere, vmem],
        out_shape=[
            jax.ShapeDtypeStruct((M, F, X, Y), F32),
            jax.ShapeDtypeStruct((copies, 16, 128), F32),
        ],
        scratch_shapes=[
            pltpu.VMEM((M, F, X, Y), F32),
            pltpu.VMEM((F, KX, Y), BF16),
            pltpu.VMEM((F, KX, Y), BF16),
            pltpu.VMEM((PAIRS, HALO, Y), F32),
            pltpu.VMEM((PAIRS, HALO, Y), F32),
            pltpu.VMEM((2 * (KX + MX), 2 * MX), F32),
            pltpu.SemaphoreType.DMA((4, PAIRS)),
            pltpu.SemaphoreType.DMA((2,)),
        ],
        cost_estimate=pl.CostEstimate(
            flops=8 * 10**9, bytes_accessed=14 * 10**6, transcendentals=0
        ),
        name="halo",
    )(a, p_hi, p_lo, before, after, cb, ca, weights, gp)


def pair_total(ref):
    hi, lo = ref[0, 0:8, :], ref[0, 8:16, :]
    for i in range(1, ref.shape[0]):
        hi, err = two_sum(hi, ref[i, 0:8, :])
        lo = lo + ref[i, 8:16, :] + err
    return hi, lo


def middle_kernel(in_ref, out_ref):
    hi, lo = pair_total(in_ref)
    hi, lo = two_sum(hi, lo)
    for i in range(out_ref.shape[0]):
        out_ref[i, 0:8, :] = hi
        out_ref[i, 8:16, :] = lo


def middle(lines, copies):
    return pl.pallas_call(
        middle_kernel,
        out_shape=jax.ShapeDtypeStruct((copies, 16, 128), F32),
        name="middle",
    )(lines)


def sent_to_all(copies, axis):
    return lax.all_to_all(copies, axis, split_axis=0, concat_axis=0, tiled=True)


def grid_of(v, top):
    return (v + top) - top


def slices(hi, lo, axis):
    top = jnp.max(jnp.abs(hi), axis=axis, keepdims=True)
    first = grid_of(hi, top * 2.0**16)
    rest = hi - first
    second = grid_of(rest, top * 2.0**8)
    return first, second, (rest - second) + lo


def pair_dot(a, b, dims):
    a1, a2, a3 = slices(*a, dims[0][0][0])
    b1, b2, b3 = slices(*b, dims[0][1][0])
    dot = functools.partial(exact_dot, dims=dims)
    big = dot(a1, b1)
    mid = dot(a1, b2) + dot(a2, b1)
    low = dot(a1, b3) + dot(a2, b2 + b3) + dot(a3, b1 + b2)
    big, err = two_sum(big, mid)
    return two_sum(big, err + low)


def pair_add(a, b):
    big, err = two_sum(a[0], b[0])
    return two_sum(big, err + (a[1] + b[1]))


def factor(gram):
    n = gram.shape[0]
    row, lane = iota((n, 128), 0), iota((n, 128), 1)
    eye = (iota((n, n), 0) == iota((n, n), 1)).astype(F32)
    t = jnp.concatenate([gram, eye, jnp.zeros((n, 128 - 2 * n), F32)], axis=1)
    pivots = jnp.zeros((n, 128), F32)
    for k in range(n):
        column = jnp.broadcast_to(t[:, k : k + 1], (n, 128))
        pivot = jnp.broadcast_to(column[k : k + 1, :], (n, 128))
        line = jnp.broadcast_to(t[k : k + 1, :], (n, 128))
        pivots = jnp.where(row == k, pivot, pivots)
        t = t - where0(row > k, column / pivot) * line
    t = t / jnp.sqrt(pivots)
    upper = where0(row <= lane, t)[:, 0:n]
    return upper, t[:, n : 2 * n]


def final_kernel(
    line_ref, a_hbm, hi_hbm, lo_hbm, out_hbm, proj_ref, tri_ref,
    a, p_hi, p_lo, out, table, mp, in_sems, out_sems, *, cells,
):
    gets = [
        pltpu.make_async_copy(src, dst, in_sems.at[i])
        for i, (src, dst) in enumerate(((a_hbm, a), (hi_hbm, p_hi), (lo_hbm, p_lo)))
    ]
    for get in gets:
        get.start()

    hi, lo = pair_total(line_ref)
    hi, lo = two_sum(hi, lo)
    odd = cells
    while odd % 2 == 0:
        odd //= 2
    scale = float(odd) / float(cells)
    guess = hi / float(odd)
    big = guess * 4097.0
    big = big - (big - guess)
    left = ((hi - big * float(odd)) - (guess - big) * float(odd)) + lo
    hi, lo = two_sum(guess, left / float(odd))
    hi, lo = hi * scale, lo * scale

    lane8 = iota((8, 128), 1)

    def unpack(v):
        rows = [roll(v, -16 * i, 1) for i in range(5)]
        top = where0(lane8 < 24, roll(v, -80, 1))
        centre = where0((lane8 >= 8) & (lane8 < 24), roll(v, -96, 1))
        end = where0((lane8 >= 16) & (lane8 < 24), roll(v, -104, 1))
        upper = jnp.concatenate([top, centre, end], axis=0)[:, 0:K]
        off = where0(iota((K, K), 1) // 8 > iota((K, K), 0) // 8, upper)
        eye = (iota((K, K), 0) == iota((K, K), 1)).astype(F32)
        return (
            jnp.concatenate(rows[0:3], axis=0)[:, 0:M],
            jnp.concatenate(rows[3:5], axis=0)[:, 0:M],
            upper + exact_dot(eye, off, NT),
        )

    (c_hi, s_hi, g_hi), (c_lo, s_lo, g_lo) = unpack(hi), unpack(lo)
    zero = jnp.zeros((K, M), F32)
    second = c_hi - exact_dot(g_hi, c_hi)
    proj = c_hi + second
    eye = (iota((K, K), 0) == iota((K, K), 1)).astype(F32)
    proj_ref[...] = exact_dot(proj, eye, TN)
    gp = pair_dot((g_hi, g_lo), (proj, zero), NN)
    t_hi, t_lo = pair_add(gp, (-c_hi, -c_lo))
    gram = pair_dot(
        (jnp.concatenate([proj, c_hi], axis=0), jnp.concatenate([zero, c_lo], axis=0)),
        (jnp.concatenate([t_hi, -proj], axis=0), jnp.concatenate([t_lo, zero], axis=0)),
        TN,
    )
    gram = pair_add((s_hi, s_lo), gram)
    upper_one, inv_one = factor(gram[0])
    none = jnp.zeros((M, M), F32)
    again = pair_dot((inv_one, none), gram, NN)
    again = pair_dot(again, (inv_one, none), NT)
    upper_two, inv_two = factor(again[0] + again[1])
    tri_ref[...] = exact_dot(upper_two, upper_one)
    mix = exact_dot(inv_two, inv_one)
    mix_p = -exact_dot(mix, proj, NT)

    rows = exact_dot((iota((MX, M), 0) // X == iota((MX, M), 1)).astype(F32), mix)
    for j in range(M):
        table[j] = jnp.broadcast_to(rows[:, j : j + 1], (MX, 128))
    row, col = iota((MX, KX), 0), iota((MX, KX), 1)
    n1, n2 = split2(where0(row % X == col % X, spread(mix_p, MX, KX)))
    mp[...] = jnp.concatenate([n1, n2, n1], axis=1)
    for get in gets:
        get.wait()

    def put(q):
        at = pl.ds(2 * q, 2)
        return pltpu.make_async_copy(out.at[:, at], out_hbm.at[:, at], out_sems.at[q])

    def two(q, carry):
        for i in range(2):
            f = 2 * q + i
            p1 = p_hi[f]
            both = half_dot(mp[...], jnp.concatenate([p1, p1, p_lo[f]], axis=0))
            for h in range(2):
                half = slice(h * 128, (h + 1) * 128)
                parts = [a[j, f, :, half] for j in range(M)]
                for k in range(M):
                    at = slice(k * X, (k + 1) * X)
                    total = table[0, at, :] * parts[0]
                    for j in range(1, k + 1):
                        total = total + table[j, at, :] * parts[j]
                    out[k, f, :, half] = total + both[at, half]
        put(q).start()
        return carry

    lax.fori_loop(0, TWO, two, 0)

    def end(q, carry):
        put(q).wait()
        return carry

    lax.fori_loop(0, TWO, end, 0)


def final(lines, a, p_hi, p_lo, cells):
    vmem = pl.BlockSpec(memory_space=pltpu.VMEM)
    anywhere = pl.BlockSpec(memory_space=pl.ANY)
    return pl.pallas_call(
        functools.partial(final_kernel, cells=cells),
        in_specs=[vmem, anywhere, anywhere, anywhere],
        out_specs=[anywhere, vmem, vmem],
        out_shape=[
            jax.ShapeDtypeStruct((M, F, X, Y), F32),
            jax.ShapeDtypeStruct((M, K), F32),
            jax.ShapeDtypeStruct((M, M), F32),
        ],
        scratch_shapes=[
            pltpu.VMEM((M, F, X, Y), F32),
            pltpu.VMEM((F, KX, Y), BF16),
            pltpu.VMEM((F, KX, Y), BF16),
            pltpu.VMEM((M, F, X, Y), F32),
            pltpu.VMEM((M, MX, 128), F32),
            pltpu.VMEM((MX, 3 * KX), BF16),
            pltpu.SemaphoreType.DMA((3,)),
            pltpu.SemaphoreType.DMA((TWO,)),
        ],
        name="final",
    )(lines, a, p_hi, p_lo)


def on_device(
    krylov_block, prior_basis, flux_along, flux_across, collision, field_rates, wall_table,
    wall_mask, wall_type,
):
    cells = F * X * lax.axis_size(GX) * Y * lax.axis_size(GY)
    first, last = pack(krylov_block)

    def onward(axis):
        return [(i, i + 1) for i in range(lax.axis_size(axis) - 1)]

    def back(axis):
        return [(j, i) for i, j in onward(axis)]

    before = lax.ppermute(last, GX, onward(GX))
    after = lax.ppermute(first, GX, back(GX))
    applied, yfirst, ylast, weights = inside(
        krylov_block, flux_along, flux_across, collision, wall_mask, wall_type, field_rates,
        wall_table,
    )
    ybefore = lax.ppermute(ylast, GY, onward(GY))
    yafter = lax.ppermute(yfirst, GY, back(GY))
    gp, p_hi, p_lo = basis(prior_basis)
    cb, ca = columns(ybefore, yafter, flux_across)
    sizes = [lax.axis_size(stage) for stage in STAGES]
    applied, lines = with_halo(
        applied, p_hi, p_lo, before, after, cb, ca, weights, gp, sizes[0]
    )
    lines = middle(sent_to_all(lines, STAGES[0]), sizes[1])
    lines = sent_to_all(lines, STAGES[1])
    new_block, projection, triangle = final(lines, applied, p_hi, p_lo, cells)
    return new_block, projection.T, triangle


def solution(mesh):
    torus = Mesh(mesh.devices.reshape(8, 4, 4, 2), ("gx_z", "gx_x", "gy_y", "gy_c"))
    cells = P(GX, GY)
    stack = P(None, None, GX, GY)
    in_specs = (stack, stack, P(), P(), cells, P(), P(), cells, cells)
    out_specs = (stack, P(), P())
    return jax.shard_map(
        on_device, mesh=torus, in_specs=in_specs, out_specs=out_specs, check_vma=False
    )
```

time: 112 us -> 109 us (0.973)
  Pallas kernels: 61.4 us -> 58.6 us
    pallas_call x3 -> x4, Pallas kernels: 44.4 us -> 39.6 us  [the longest x1 16.1 us: final(): pl.pallas_call(functools.partial(final_kernel, cells=cells), in_specs=[vm...]
    pallas_call x1, Pallas kernels: 10.7 us -> 13.2 us  [inside(): pl.pallas_call(functools.partial(inside_kernel, step_m=step_m), grid=(M /...]
    pallas_call x1 -> x0, local copies, waits for them, and re-layouts: 1.38 us -> none  [final(): pl.pallas_call(functools.partial(final_kernel, cells=cells, parts=parts),...]
  transfers between devices with their start and end apart: 4 -> 4, of which waited for: 0 -> 0; matrix products, arithmetic and copies ran while one was open for 0% -> 0% of each run, Pallas kernels for 19% -> 22%
where the time goes in v1:
time: 109 us; the launch traced here: 108 us
  Pallas kernels  58.6 us (54%)
  blocking collectives  35 us (32%)
  starting transfers between devices  11.2 us (10%)
  local copies, waits for them, and re-layouts  2.51 us (2%)
    all_to_all x2, blocking collectives, sent_to_all(): return lax.all_to_all(copies, axis, split_axis=0, concat_axis=0, tiled=True)  35 us
    pallas_call x1, Pallas kernels, final(): pl.pallas_call(functools.partial(final_kernel, cells=cells), in_specs=[vm...  16.1 us
    pallas_call x1, Pallas kernels, inside(): pl.pallas_call(functools.partial(inside_kernel, step_m=step_m), grid=(M /...  13.2 us
    pallas_call x1, Pallas kernels, with_halo(): pl.pallas_call(halo_kernel, in_specs=[anywhere] * 5 + [vmem] * 4, out_spe...  12.9 us
    pallas_call x1, Pallas kernels, basis(): pl.pallas_call(basis_kernel, in_specs=[anywhere], out_specs=[pl.BlockSpec...  7.78 us
    pallas_call x1, Pallas kernels, pack(): pl.pallas_call(functools.partial(pack_kernel, step_m=step_m), grid=(M //...  4.26 us
    ppermute x1, starting transfers between devices, on_device(): ybefore = lax.ppermute(ylast, GY, onward(GY))  4.03 us
    ppermute x1, starting transfers between devices, on_device(): before = lax.ppermute(last, GX, onward(GX))  3.97 us
  transfers between devices with their start and end apart: 4, of which 0 were waited for; matrix products, arithmetic and copies ran while one was open for 0% of the time, Pallas kernels for 22%

profile of v1, /device:TPU:1, one launch (start us, length us, event | category | flops | bytes accessed | tf_op | source)
XLA Modules:
  0.0 108.0 jit_solution(10949728939477122485)
XLA Ops:
  0.6 4.3 %pack.1 = (f32[8,104,256]{2,1,0:T(8,128)}, f32[8,104,256]{2,1,0:T(8,128)}) custom-call(f32[16,26,8,256]{3,2,1,0:T(8,128)} %v_ref.3), custom_call_target="tpu_custom_call" | custom-call | flops 1000000 | bytes 6000000 | tf_op jit(solution)/shard_map/pack/pallas_call | solution.py:91
  4.9 4.0 %collective-permute-start = (f32[8,104,256]{2,1,0:T(8,128)}, f32[8,104,256]{2,1,0:T(8,128)S(1)}, u32[]{:S(2)}, u32[]{:S(2)}) collective-permute-start(f32[8,104,256]{2,1,0:T(8,128)} %get-tuple-element.22), channel_id=1, source_target_pairs={{0,8},{8,16},{16,24},{24,32},{32,40},{40,48},{48,56},{56,64},{64,7... | collective-permute-start | bytes 2555912 | tf_op jit(solution)/shard_map/ppermute | solution.py:657
  8.9 1.3 %collective-permute-start.1 = (f32[8,104,256]{2,1,0:T(8,128)}, f32[8,104,256]{2,1,0:T(8,128)S(1)}, u32[]{:S(2)}, u32[]{:S(2)}) collective-permute-start(f32[8,104,256]{2,1,0:T(8,128)} %get-tuple-element.23), channel_id=1, source_target_pairs={{8,0},{16,8},{24,16},{32,24},{40,32},{48,40},{56,48},{64,56},{72,6... | collective-permute-start | bytes 2555912 | tf_op jit(solution)/shard_map/ppermute | solution.py:658
  10.2 13.2 %inside.1 = (f32[16,26,8,256]{3,2,1,0:T(8,128)}, f32[208,128]{1,0:T(8,128)}, f32[208,128]{1,0:T(8,128)}, bf16[2,208,208]{2,1,0:T(8,128)(2,1)}) custom-call(f32[16,26,8,256]{3,2,1,0:T(8,128)} %v_ref.3, f32[26,26]{1,0:T(8,128)} %along_ref.1, f32[26,26]{1,0:T(8,128)} %across_ref.3, f32[8,256]{1,0:T(8,128)} %coll_ref.1, s32[8,256]{1,0:T(8,128)} %mask_ref.1, ...), custom_call_target="tpu_custom_call" | custom-call | flops 8000000000 | bytes 7000000 | tf_op jit(solution)/shard_map/inside/pallas_call | solution.py:179
  23.4 4.0 %collective-permute-start.2 = (f32[208,128]{1,0:T(8,128)}, f32[208,128]{1,0:T(8,128)S(1)}, u32[]{:S(2)}, u32[]{:S(2)}) collective-permute-start(f32[208,128]{1,0:T(8,128)} %get-tuple-element.24), channel_id=1, source_target_pairs={{0,1},{1,2},{2,3},{3,4},{4,5},{5,6},{6,7},{8,9},{9,10},{10,11},{11... | collective-permute-start | bytes 319496 | tf_op jit(solution)/shard_map/ppermute | solution.py:663
  27.4 1.9 %collective-permute-start.3 = (f32[208,128]{1,0:T(8,128)}, f32[208,128]{1,0:T(8,128)S(1)}, u32[]{:S(2)}, u32[]{:S(2)}) collective-permute-start(f32[208,128]{1,0:T(8,128)} %get-tuple-element.25), channel_id=1, source_target_pairs={{1,0},{2,1},{3,2},{4,3},{5,4},{6,5},{7,6},{9,8},{10,9},{11,10},{12... | collective-permute-start | bytes 319496 | tf_op jit(solution)/shard_map/ppermute | solution.py:664
  29.3 7.8 %basis.1 = (f32[16,128]{1,0:T(8,128)}, bf16[26,192,256]{2,1,0:T(8,128)(2,1)}, bf16[26,192,256]{2,1,0:T(8,128)(2,1)}) custom-call(f32[24,26,8,256]{3,2,1,0:T(8,128)} %p_hbm.1), custom_call_target="tpu_custom_call" | custom-call | flops 8000000000 | bytes 10000000 | tf_op jit(solution)/shard_map/basis/pallas_call | solution.py:309
  37.1 0.0 collective-permute-done.2.ybefore_ref
  37.1 0.0 copy-start.2
  37.1 0.0 collective-permute-done.3.yafter_ref
  37.1 0.6 copy-done.2
  37.8 0.0 copy-start.3
  37.8 0.6 copy-done.3
  38.4 2.8 %columns.1 = (f32[208,128]{1,0:T(8,128)}, f32[208,128]{1,0:T(8,128)}) custom-call(f32[208,128]{1,0:T(8,128)} %copy-done.2, f32[208,128]{1,0:T(8,128)} %copy-done.3, f32[26,26]{1,0:T(8,128)} %across_ref.3), custom_call_target="tpu_custom_call" | custom-call | flops 100000000 | bytes 1000000 | tf_op jit(solution)/shard_map/columns/pallas_call | solution.py:224
  41.2 0.0 collective-permute-done.before_hbm
  41.2 0.0 collective-permute-done.1.after_hbm
  41.2 0.0 copy-start.1
  41.2 1.0 copy-done
  42.2 0.3 copy-done.1
  42.5 12.9 %halo.1 = (f32[16,26,8,256]{3,2,1,0:T(8,128)}, f32[16,16,128]{2,1,0:T(8,128)}) custom-call(f32[16,26,8,256]{3,2,1,0:T(8,128)} %get-tuple-element.19.a_hbm, bf16[26,192,256]{2,1,0:T(8,128)(2,1)} %get-tuple-element.20.hi_hbm, bf16[26,192,256]{2,1,0:T(8,128)(2,1)} %get-tuple-element.21.lo_hbm, f32[8,104,256]{2,1,0:T(8,128)} %copy-done, ...), custom_call_target="tpu_custom_call" | custom-call | flops 8000000000 | bytes 14000000 | tf_op jit(solution)/shard_map/halo/pallas_call | solution.py:418
  55.4 14.4 %all_to_all.10.in_ref = f32[16,16,128]{2,1,0:T(8,128)} all-to-all(f32[16,16,128]{2,1,0:T(8,128)} %get-tuple-element.30), channel_id=1, replica_groups=mesh['gx_z'=8,'gx_x'=4,'gy_y'=4,'gy_c'=2] {'gx_x','gy_y'}, dimensions={0} | all-to-all | bytes 262144 | tf_op jit(solution)/shard_map/all_to_all | solution.py:468
  69.8 1.6 %middle.1 = f32[16,16,128]{2,1,0:T(8,128)} custom-call(f32[16,16,128]{2,1,0:T(8,128)} %all_to_all.10.in_ref), custom_call_target="tpu_custom_call" | custom-call | tf_op jit(solution)/shard_map/middle/pallas_call | solution.py:460
  71.4 20.6 %all_to_all.11.line_ref = f32[16,16,128]{2,1,0:T(8,128)} all-to-all(f32[16,16,128]{2,1,0:T(8,128)} %middle.1), channel_id=1, replica_groups=mesh['gx_z'=8,'gx_x'=4,'gy_y'=4,'gy_c'=2] {'gx_z','gy_c'}, dimensions={0} | all-to-all | bytes 262144 | tf_op jit(solution)/shard_map/all_to_all | solution.py:468
  92.0 16.1 %final.1 = (f32[16,26,8,256]{3,2,1,0:T(8,128)}, f32[16,24]{1,0:T(8,128)}, f32[16,16]{1,0:T(8,128)}) custom-call(f32[16,16,128]{2,1,0:T(8,128)} %all_to_all.11.line_ref, f32[16,26,8,256]{3,2,1,0:T(8,128)} %get-tuple-element.31.a_hbm, bf16[26,192,256]{2,1,0:T(8,128)(2,1)} %get-tuple-element.20.hi_hbm, bf16[26,192,256]{2,1,0:T(8,128)(2,1)} %get-tuple-element.21.lo_hbm), custom_call_target="tpu_custom_call" | custom-call | tf_op jit(solution)/shard_map/final/pallas_call | solution.py:621
  (1 shorter events, 0.0 us)
Async XLA Ops:
  4.9 36.3 %collective-permute-start = (f32[8,104,256]{2,1,0:T(8,128)}, f32[8,104,256]{2,1,0:T(8,128)S(1)}, u32[]{:S(2)}, u32[]{:S(2)}) collective-permute-start(f32[8,104,256]{2,1,0:T(8,128)} %get-tuple-element.22), channel_id=1, source_target_pairs={{0,8},{8,16},{16,24},{24,32},{32,40},{40,48},{48,56},{56,64},{64,7... | collective-permute-start | bytes 2555912 | tf_op jit(solution)/shard_map/ppermute | solution.py:657
  8.9 32.3 %collective-permute-start.1 = (f32[8,104,256]{2,1,0:T(8,128)}, f32[8,104,256]{2,1,0:T(8,128)S(1)}, u32[]{:S(2)}, u32[]{:S(2)}) collective-permute-start(f32[8,104,256]{2,1,0:T(8,128)} %get-tuple-element.23), channel_id=1, source_target_pairs={{8,0},{16,8},{24,16},{32,24},{40,32},{48,40},{56,48},{64,56},{72,6... | collective-permute-start | bytes 2555912 | tf_op jit(solution)/shard_map/ppermute | solution.py:658
  23.4 13.8 %collective-permute-start.2 = (f32[208,128]{1,0:T(8,128)}, f32[208,128]{1,0:T(8,128)S(1)}, u32[]{:S(2)}, u32[]{:S(2)}) collective-permute-start(f32[208,128]{1,0:T(8,128)} %get-tuple-element.24), channel_id=1, source_target_pairs={{0,1},{1,2},{2,3},{3,4},{4,5},{5,6},{6,7},{8,9},{9,10},{10,11},{11... | collective-permute-start | bytes 319496 | tf_op jit(solution)/shard_map/ppermute | solution.py:663
  27.4 9.7 %collective-permute-start.3 = (f32[208,128]{1,0:T(8,128)}, f32[208,128]{1,0:T(8,128)S(1)}, u32[]{:S(2)}, u32[]{:S(2)}) collective-permute-start(f32[208,128]{1,0:T(8,128)} %get-tuple-element.25), channel_id=1, source_target_pairs={{1,0},{2,1},{3,2},{4,3},{5,4},{6,5},{7,6},{9,8},{10,9},{11,10},{12... | collective-permute-start | bytes 319496 | tf_op jit(solution)/shard_map/ppermute | solution.py:664
  37.1 0.7 copy-start.2
  37.8 0.6 copy-start.3
  41.2 1.0 copy-start
  41.2 1.2 %copy-start.1 = (f32[8,104,256]{2,1,0:T(8,128)}, f32[8,104,256]{2,1,0:T(8,128)S(1)}, u32[]{:S(2)}) copy-start(f32[8,104,256]{2,1,0:T(8,128)S(1)} %collective-permute-done.1.after_hbm) | copy-start | bytes 2555908

commit v2 on v1

--- a/solution.py
+++ b/solution.py
@@ -79,21 +79,61 @@
     return pltpu.roll(v, shift % size if isinstance(shift, int) else shift, axis)
 
 
-def pack_kernel(v_ref, first_ref, last_ref, *, step_m):
-    for i in range(step_m):
-        for f in range(F):
-            at = (i % 2 * F + f) * 2
-            first_ref[i // 2, at : at + 2, :] = v_ref[i, f, 0:2, :]
-            last_ref[i // 2, at : at + 2, :] = v_ref[i, f, X - 2 : X, :]
-
-
-def pack(v, step_m=4):
+def moved(v, shift):
+    lane = iota((v.shape[0], 128), 1)
+    left, right = roll(v[:, 0:128], shift, 1), roll(v[:, 128:], shift, 1)
+    if shift > 0:
+        left, right = where0(lane >= shift, left), jnp.where(lane >= shift, right, left)
+    else:
+        keep = lane < 128 + shift
+        left, right = jnp.where(keep, left, right), where0(keep, right)
+    return jnp.concatenate([left, right], axis=1)
+
+
+def pack_kernel(v_hbm, first_hbm, last_hbm, v, first, last, sems):
+    def get(q):
+        at = pl.ds(2 * q, 2)
+        return pltpu.make_async_copy(v_hbm.at[at], v.at[at], sems.at[0, q])
+
+    def puts(q):
+        return (
+            pltpu.make_async_copy(first.at[q], first_hbm.at[q], sems.at[1, q]),
+            pltpu.make_async_copy(last.at[q], last_hbm.at[q], sems.at[2, q]),
+        )
+
+    for q in range(PAIRS):
+        get(q).start()
+
+    def pair(q, carry):
+        get(q).wait()
+        for i in range(2):
+            for f in range(F):
+                at = (i * F + f) * 2
+                first[q, at : at + 2, :] = v[2 * q + i, f, 0:2, :]
+                last[q, at : at + 2, :] = v[2 * q + i, f, X - 2 : X, :]
+        for put in puts(q):
+            put.start()
+        return carry
+
+    lax.fori_loop(0, PAIRS, pair, 0)
+    for q in range(PAIRS):
+        for put in puts(q):
+            put.wait()
+
+
+def pack(v):
+    anywhere = pl.BlockSpec(memory_space=pl.ANY)
     return pl.pallas_call(
-        functools.partial(pack_kernel, step_m=step_m),
-        grid=(M // step_m,),
-        in_specs=[pl.BlockSpec((step_m, F, X, Y), lambda i: (i, 0, 0, 0))],
-        out_specs=[pl.BlockSpec((step_m // 2, HALO, Y), lambda i: (i, 0, 0))] * 2,
+        pack_kernel,
+        in_specs=[anywhere],
+        out_specs=[anywhere] * 2,
         out_shape=[jax.ShapeDtypeStruct((PAIRS, HALO, Y), F32)] * 2,
+        scratch_shapes=[
+            pltpu.VMEM((M, F, X, Y), F32),
+            pltpu.VMEM((PAIRS, HALO, Y), F32),
+            pltpu.VMEM((PAIRS, HALO, Y), F32),
+            pltpu.SemaphoreType.DMA((3, PAIRS)),
+        ],
         cost_estimate=pl.CostEstimate(flops=10**6, bytes_accessed=6 * 10**6, transcendentals=0),
         name="pack",
     )(v)
@@ -101,24 +141,31 @@
 
 def inside_kernel(
     v_ref, along_ref, across_ref, coll_ref, mask_ref, type_ref, rate_ref, table_ref,
-    out_ref, yfirst_ref, ylast_ref, halo_ref, w, coeff, *, step_m,
+    out_ref, yfirst_ref, ylast_ref, halo_ref, ycol_ref, w, coeff, *, step_m,
 ):
     @pl.when(pl.program_id(0) == 0)
     def _():
+        eye = (iota((F, F), 0) == iota((F, F), 1)).astype(F32)
+        along, across = 0.5 * along_ref[...], 0.5 * across_ref[...]
+        plus, minus = along - 4.0 * DAMP * eye, -along - 4.0 * DAMP * eye
+        halves = [h for v in (plus, minus, across) for h in split2(v)]
+        left = (iota((FX, F), 0) // X == iota((FX, F), 1)).astype(BF16)
+        right = (iota((F, FX), 1) // X == iota((F, FX), 0)).astype(BF16)
+        tall = [half_dot(left, h).astype(BF16) for h in halves]
+        plus_hi, plus_lo, minus_hi, minus_lo, across_hi, across_lo = (
+            half_dot(v, right) for v in tall
+        )
         row, col = iota((FX, FX), 0), iota((FX, FX), 1)
-        same_f = row // X == col // X
         step = col % X - row % X
-        fa = spread(along_ref[...], FX, FX)
-        fc = spread(across_ref[...], FX, FX)
-        wx = where0(step == 1, 0.5 * fa) - where0(step == -1, 0.5 * fa)
-        near = same_f & (jnp.abs(step) == 1)
-        far = same_f & (jnp.abs(step) == 2)
-        wx = wx + jnp.where(near, -4.0 * DAMP, 0.0) + jnp.where(far, DAMP, 0.0)
-        wy = where0(step == 0, 0.5 * fc)
-        for i, part in enumerate((wx, wy)):
-            hi, lo = split2(part)
-            w[0, i * FX : (i + 1) * FX, :] = hi
-            w[1, i * FX : (i + 1) * FX, :] = lo
+        far = (row // X == col // X) & (jnp.abs(step) == 2)
+        hi = where0(step == 1, plus_hi) + where0(step == -1, minus_hi) + jnp.where(far, DAMP, 0.0)
+        lo = where0(step == 1, plus_lo) + where0(step == -1, minus_lo)
+        yhi, ylo = where0(step == 0, across_hi), where0(step == 0, across_lo)
+        hi = jnp.concatenate([hi, yhi], axis=0)
+        lo = jnp.concatenate([lo, ylo], axis=0)
+        w[...] = jnp.concatenate([hi, lo, hi], axis=1).astype(BF16)
+        ycol_ref[0] = yhi.astype(BF16)
+        ycol_ref[1] = ylo.astype(BF16)
         walls = [
             jnp.where(type_ref[...] == t, mask_ref[...].astype(F32), 0.0)
             for t in range(table_ref.shape[0])
@@ -132,45 +179,43 @@
         row, col = iota((FX, HALO), 0), iota((FX, HALO), 1)
         x, f = row % X, row // X
         g, j, later = col % (2 * F) // 2, col % 2, col >= 2 * F
-        left = (iota((FX, F), 0) // X == iota((FX, F), 1)).astype(F32)
-        right = (iota((F, HALO), 1) % (2 * F) // 2 == iota((F, HALO), 0)).astype(F32)
-        fa = 0.5 * exact_dot(exact_dot(left, along_ref[...]), right)
-        same = f == g
+        right = (iota((F, HALO), 1) % (2 * F) // 2 == iota((F, HALO), 0)).astype(BF16)
+        plus_hi, plus_lo, minus_hi, minus_lo = (half_dot(v, right) for v in tall[:4])
         edge_b = (x == 0) & (j == 1) & ~later
         edge_a = (x == X - 1) & (j == 0) & later
-        wh = where0(edge_a, fa) - where0(edge_b, fa)
-        wh = wh + jnp.where(same & (edge_a | edge_b), -4.0 * DAMP, 0.0)
         outer = ((x == j) & ~later) | ((x == X - 2 + j) & later)
-        wh = wh + jnp.where(same & outer, DAMP, 0.0)
-        hi = wh.astype(BF16).astype(F32)
+        hi = where0(edge_a, plus_hi) + where0(edge_b, minus_hi)
+        hi = hi + jnp.where((f == g) & outer, DAMP, 0.0)
+        lo = where0(edge_a, plus_lo) + where0(edge_b, minus_lo)
         halo_ref[0] = jnp.concatenate([hi, hi], axis=1).astype(BF16)
-        halo_ref[1] = jnp.concatenate([wh - hi, jnp.zeros_like(wh)], axis=1).astype(BF16)
+        halo_ref[1] = jnp.concatenate([lo, jnp.zeros_like(lo)], axis=1).astype(BF16)
         yfirst_ref[...] = jnp.zeros_like(yfirst_ref)
         ylast_ref[...] = jnp.zeros_like(ylast_ref)
 
-    lane = iota((FX, Y), 1)
     lane2 = iota((FX, 128), 1) // 2
 
-    def one(i, carry):
+    def one(i):
         m = pl.program_id(0) * step_m + i
         v = v_ref[i].reshape(FX, Y)
         mine = lane2 == m
         yfirst_ref[...] = jnp.where(mine, roll(v[:, 0:128], 2 * m, 1), yfirst_ref[...])
         ylast_ref[...] = jnp.where(mine, roll(v[:, Y - 128 :], 2 * m + 2, 1), ylast_ref[...])
         hi, lo = split2(v)
-        left = jnp.concatenate([w[0], w[1], w[0]], axis=1)
-        both = half_dot(left, jnp.concatenate([hi, hi, lo], axis=0))
+        both = half_dot(w[...], jnp.concatenate([hi, hi, lo], axis=0))
         u = both[FX:]
         out = both[:FX] + coeff[...] * v
         side = 4.0 * DAMP * v
-        out = out + where0(lane < Y - 1, roll(u - side, -1, 1))
-        out = out - where0(lane > 0, roll(u + side, 1, 1))
         two = DAMP * v
-        out = out + where0(lane < Y - 2, roll(two, -2, 1)) + where0(lane > 1, roll(two, 2, 1))
+        out = out + moved(u - side, -1) - moved(u + side, 1)
+        out = out + moved(two, -2) + moved(two, 2)
         out_ref[i] = out.reshape(F, X, Y)
+
+    def couple(i, carry):
+        one(2 * i)
+        one(2 * i + 1)
         return carry
 
-    lax.fori_loop(0, step_m, one, 0)
+    lax.fori_loop(0, step_m // 2, couple, 0)
 
 
 def inside(v, along, across, coll, mask, types, rates, table, step_m=4):
@@ -194,14 +239,16 @@
             pl.BlockSpec((FX, 128), whole2),
             pl.BlockSpec((FX, 128), whole2),
             pl.BlockSpec((2, FX, 2 * HALO), lambda i: (0, 0, 0)),
+            pl.BlockSpec((2, FX, FX), lambda i: (0, 0, 0)),
         ],
         out_shape=[
             jax.ShapeDtypeStruct((M, F, X, Y), F32),
             jax.ShapeDtypeStruct((FX, 128), F32),
             jax.ShapeDtypeStruct((FX, 128), F32),
             jax.ShapeDtypeStruct((2, FX, 2 * HALO), BF16),
-        ],
-        scratch_shapes=[pltpu.VMEM((2, 2 * FX, FX), BF16), pltpu.VMEM((FX, Y), F32)],
+            jax.ShapeDtypeStruct((2, FX, FX), BF16),
+        ],
+        scratch_shapes=[pltpu.VMEM((2 * FX, 3 * FX), BF16), pltpu.VMEM((FX, Y), F32)],
         cost_estimate=pl.CostEstimate(
             flops=8 * 10**9, bytes_accessed=7 * 10**6, transcendentals=0
         ),
@@ -209,82 +256,57 @@
     )(v, along, across, coll, mask, types, rates, table)
 
 
-def columns_kernel(ybefore_ref, yafter_ref, across_ref, cb_ref, ca_ref):
-    full = iota((FX, FX), 1) % X == iota((FX, FX), 0) % X
-    wy = where0(full, 0.5 * spread(across_ref[...], FX, FX))
-    lane = iota((FX, 128), 1)
-    yb, ya = ybefore_ref[...], yafter_ref[...]
-    term = exact_dot(wy, yb) + 4.0 * DAMP * yb
-    cb_ref[...] = DAMP * yb - where0(lane % 2 == 0, roll(term, -1, 1))
-    term = exact_dot(wy, ya) - 4.0 * DAMP * ya
-    ca_ref[...] = DAMP * ya + where0(lane % 2 == 1, roll(term, 1, 1))
-
-
-def columns(ybefore, yafter, across):
-    return pl.pallas_call(
-        columns_kernel,
-        out_shape=[jax.ShapeDtypeStruct((FX, 128), F32)] * 2,
-        cost_estimate=pl.CostEstimate(flops=10**8, bytes_accessed=10**6, transcendentals=0),
-        name="columns",
-    )(ybefore, yafter, across)
-
-
 def diagonal(big, small, left, right):
     rows, cols = left * X, right * X
     own = iota((rows, cols), 0) % X == iota((rows, cols), 1) % X
-    pick = (iota((cols, 128), 0) // X == iota((cols, 128), 1)).astype(F32)
-    big = exact_dot(where0(own, big), pick)
-    small = exact_dot(where0(own, small), pick)
-    big, small = big.reshape(left, X, 128), small.reshape(left, X, 128)
+    big = jnp.sum(where0(own, big).reshape(left, X, cols), axis=1)
+    small = jnp.sum(where0(own, small).reshape(left, X, cols), axis=1)
     for shift in (4, 2, 1):
-        big, err = two_sum(big, roll(big, shift, 1))
-        small = small + roll(small, shift, 1) + err
-    sel = (iota((left, rows), 1) == X * iota((left, rows), 0)).astype(F32)
-    return exact_dot(sel, big.reshape(rows, 128)), exact_dot(sel, small.reshape(rows, 128))
+        big, err = two_sum(big, roll(big, -shift, 1))
+        small = small + roll(small, -shift, 1) + err
+    pick = (iota((cols, 128), 0) == X * iota((cols, 128), 1)).astype(F32)
+    return exact_dot(big, pick), exact_dot(small, pick)
 
 
 TWO = F // 2
 
 
 def basis_kernel(p_hbm, out_ref, hi_hbm, lo_hbm, p, hi_ref, lo_ref, big_ref, small_ref, in_sem, out_sem):
-    def get(q):
-        return pltpu.make_async_copy(
-            p_hbm.at[:, pl.ds(2 * q, 2)], p.at[:, pl.ds(2 * q, 2)], in_sem.at[q]
-        )
+    def get(f):
+        return pltpu.make_async_copy(p_hbm.at[:, f], p.at[:, f], in_sem.at[f])
 
     def puts(q):
-        at = pl.ds(2 * q, 2)
+        at = pl.ds(TWO * q, TWO)
         return (
             pltpu.make_async_copy(hi_ref.at[at], hi_hbm.at[at], out_sem.at[0, q]),
             pltpu.make_async_copy(lo_ref.at[at], lo_hbm.at[at], out_sem.at[1, q]),
         )
 
-    for q in range(TWO):
-        get(q).start()
+    for f in range(F):
+        get(f).start()
     big_ref[...] = jnp.zeros_like(big_ref)
     small_ref[...] = jnp.zeros_like(small_ref)
 
-    def two(q, carry):
-        get(q).wait()
+    def some(q, carry):
         his, los = [], []
-        for i in range(2):
-            hi, lo = split2(p[:, 2 * q + i].reshape(KX, Y))
-            hi_ref[2 * q + i] = hi
-            lo_ref[2 * q + i] = lo
+        for i in range(TWO):
+            f = q * TWO + i
+            get(f).wait()
+            hi, lo = split2(p[:, f].reshape(KX, Y))
+            hi_ref[f] = hi
+            lo_ref[f] = lo
             his.append(hi)
             los.append(lo)
-        hi = jnp.concatenate(his, axis=1)
-        lo = jnp.concatenate(los, axis=1)
         for put in puts(q):
             put.start()
-        big_ref[...] += half_dot(hi, hi, NT)
-        half = lo * jnp.asarray(0.5, BF16)
+        half = [lo * jnp.asarray(0.5, BF16) for lo in los]
+        big_ref[...] += half_dot(jnp.concatenate(his, axis=1), jnp.concatenate(his, axis=1), NT)
         small_ref[...] += half_dot(
-            jnp.concatenate([lo, lo], axis=1), jnp.concatenate([hi, half], axis=1), NT
+            jnp.concatenate(los + los, axis=1), jnp.concatenate(his + half, axis=1), NT
         )
         return carry
 
-    lax.fori_loop(0, TWO, two, 0)
+    lax.fori_loop(0, 2, some, 0)
     hi, lo = diagonal(big_ref[...], small_ref[...], K, K)
     eye = (iota((K, K), 0) == iota((K, 128), 1)[:, 0:K]).astype(F32)
     turned = exact_dot(lo[:, 0:K], eye, TN)
@@ -296,12 +318,9 @@
         line = line + where0(lane >= 120, roll(part[16:24], 104, 1))
         out_ref[8 * half : 8 * half + 8, :] = line
 
-    def end(q, carry):
+    for q in range(2):
         for put in puts(q):
             put.wait()
-        return carry
-
-    lax.fori_loop(0, TWO, end, 0)
 
 
 def basis(p):
@@ -321,8 +340,8 @@
             pltpu.VMEM((F, KX, Y), BF16),
             pltpu.VMEM((KX, KX), F32),
             pltpu.VMEM((KX, KX), F32),
-            pltpu.SemaphoreType.DMA((TWO,)),
-            pltpu.SemaphoreType.DMA((2, TWO)),
+            pltpu.SemaphoreType.DMA((F,)),
+            pltpu.SemaphoreType.DMA((2, 2)),
         ],
         cost_estimate=pl.CostEstimate(
             flops=8 * 10**9, bytes_accessed=10 * 10**6, transcendentals=0
@@ -332,8 +351,8 @@
 
 
 def halo_kernel(
-    a_hbm, hi_hbm, lo_hbm, before_hbm, after_hbm, cb_ref, ca_ref, w_ref, gp_ref,
-    out_hbm, line_ref, a, p_hi, p_lo, before, after, acc, a_sem, sems,
+    a_hbm, hi_hbm, lo_hbm, before_hbm, after_hbm, yb_ref, ya_ref, w_ref, wy_ref, gp_ref,
+    out_hbm, line_ref, a, p_hi, p_lo, before, after, edge, acc, a_sem, sems,
 ):
     def get(q):
         at = pl.ds(2 * q, 2)
@@ -355,8 +374,15 @@
     get_hi.start()
     get_lo.start()
     lane = iota((FX, 128), 1)
-
-    def pair(q, carry):
+    yb, ya = yb_ref[...], ya_ref[...]
+    hi, lo = split2(jnp.concatenate([yb, ya], axis=1))
+    u = half_dot(wy_ref[0], hi) + half_dot(wy_ref[1], hi) + half_dot(wy_ref[0], lo)
+    term = u[:, 0:128] + 4.0 * DAMP * yb
+    edge[0] = DAMP * yb - where0(lane % 2 == 0, roll(term, -1, 1))
+    term = u[:, 128:] - 4.0 * DAMP * ya
+    edge[1] = DAMP * ya + where0(lane % 2 == 1, roll(term, 1, 1))
+
+    def pair(q):
         for each in get(q):
             each.wait()
         for i in range(2):
@@ -365,33 +391,34 @@
             h = jnp.concatenate([before[q][mine], after[q][mine]], axis=0)
             hi = h.astype(BF16).astype(F32)
             h = jnp.concatenate([hi, h - hi], axis=0).astype(BF16)
-            left = where0(lane < 2, roll(cb_ref[...], (128 - 2 * m) % 128, 1))
-            right = where0(lane >= 126, roll(ca_ref[...], 126 - 2 * m, 1))
+            left = where0(lane < 2, roll(edge[0], (128 - 2 * m) % 128, 1))
+            right = where0(lane >= 126, roll(edge[1], 126 - 2 * m, 1))
             part = a[m].reshape(FX, Y) + jnp.concatenate([left, right], axis=1)
             part = part + (half_dot(w_ref[0], h) + half_dot(w_ref[1], h))
             a[m] = part.reshape(F, X, Y)
         put(q).start()
+
+    def pairs(q, carry):
+        pair(2 * q)
+        pair(2 * q + 1)
         return carry
 
-    lax.fori_loop(0, PAIRS, pair, 0)
+    lax.fori_loop(0, PAIRS // 2, pairs, 0)
     acc[...] = jnp.zeros_like(acc)
     get_hi.wait()
     get_lo.wait()
 
-    def two(q, carry):
-        his, los, p_his, p_los = [], [], [], []
-        for i in range(2):
-            hi, lo = split2(a[:, 2 * q + i].reshape(MX, Y))
-            his.append(hi)
-            los.append(lo)
-            p_his.append(p_hi[2 * q + i])
-            p_los.append(p_lo[2 * q + i])
-        hi, lo, ph, pl_ = (jnp.concatenate(v, axis=1) for v in (his, los, p_his, p_los))
-        rows = jnp.concatenate([ph, hi, pl_, lo], axis=0)
-        acc[...] += half_dot(rows, jnp.concatenate([hi, lo], axis=0), NT)
+    def some(q, carry):
+        rows, cols = [], []
+        for i in range(TWO):
+            f = q * TWO + i
+            hi, lo = split2(a[:, f].reshape(MX, Y))
+            rows.append(jnp.concatenate([p_hi[f], hi, p_lo[f], lo], axis=0))
+            cols.append(jnp.concatenate([hi, lo], axis=0))
+        acc[...] += half_dot(jnp.concatenate(rows, axis=1), jnp.concatenate(cols, axis=1), NT)
         return carry
 
-    lax.fori_loop(0, TWO, two, 0)
+    lax.fori_loop(0, 2, some, 0)
     n = KX + MX
     big = acc[0:n, 0:MX]
     small = acc[0:n, MX:] + acc[n:, 0:MX] + acc[n:, MX:]
@@ -412,12 +439,12 @@
     lax.fori_loop(0, PAIRS, end, 0)
 
 
-def with_halo(a, p_hi, p_lo, before, after, cb, ca, weights, gp, copies):
+def with_halo(a, p_hi, p_lo, before, after, yb, ya, weights, wy, gp, copies):
     vmem = pl.BlockSpec(memory_space=pltpu.VMEM)
     anywhere = pl.BlockSpec(memory_space=pl.ANY)
     return pl.pallas_call(
         halo_kernel,
-        in_specs=[anywhere] * 5 + [vmem] * 4,
+        in_specs=[anywhere] * 5 + [vmem] * 5,
         out_specs=[anywhere, vmem],
         out_shape=[
             jax.ShapeDtypeStruct((M, F, X, Y), F32),
@@ -429,6 +456,7 @@
             pltpu.VMEM((F, KX, Y), BF16),
             pltpu.VMEM((PAIRS, HALO, Y), F32),
             pltpu.VMEM((PAIRS, HALO, Y), F32),
+            pltpu.VMEM((2, FX, 128), F32),
             pltpu.VMEM((2 * (KX + MX), 2 * MX), F32),
             pltpu.SemaphoreType.DMA((4, PAIRS)),
             pltpu.SemaphoreType.DMA((2,)),
@@ -437,15 +465,18 @@
             flops=8 * 10**9, bytes_accessed=14 * 10**6, transcendentals=0
         ),
         name="halo",
-    )(a, p_hi, p_lo, before, after, cb, ca, weights, gp)
+    )(a, p_hi, p_lo, before, after, yb, ya, weights, wy, gp)
 
 
 def pair_total(ref):
-    hi, lo = ref[0, 0:8, :], ref[0, 8:16, :]
-    for i in range(1, ref.shape[0]):
-        hi, err = two_sum(hi, ref[i, 0:8, :])
-        lo = lo + ref[i, 8:16, :] + err
-    return hi, lo
+    parts = [(ref[i, 0:8, :], ref[i, 8:16, :]) for i in range(ref.shape[0])]
+    while len(parts) > 1:
+        after = []
+        for i in range(0, len(parts) - 1, 2):
+            hi, err = two_sum(parts[i][0], parts[i + 1][0])
+            after.append((hi, parts[i][1] + parts[i + 1][1] + err))
+        parts = after + parts[len(parts) // 2 * 2 :]
+    return parts[0]
 
 
 def middle_kernel(in_ref, out_ref):
@@ -484,8 +515,9 @@
     a1, a2, a3 = slices(*a, dims[0][0][0])
     b1, b2, b3 = slices(*b, dims[0][1][0])
     dot = functools.partial(exact_dot, dims=dims)
-    big = dot(a1, b1)
-    mid = dot(a1, b2) + dot(a2, b1)
+    h1, h2, k1, k2 = (v.astype(BF16) for v in (a1, a2, b1, b2))
+    big = half_dot(h1, k1, dims)
+    mid = half_dot(h1, k2, dims) + half_dot(h2, k1, dims)
     low = dot(a1, b3) + dot(a2, b2 + b3) + dot(a3, b1 + b2)
     big, err = two_sum(big, mid)
     return two_sum(big, err + low)
@@ -501,13 +533,21 @@
     row, lane = iota((n, 128), 0), iota((n, 128), 1)
     eye = (iota((n, n), 0) == iota((n, n), 1)).astype(F32)
     t = jnp.concatenate([gram, eye, jnp.zeros((n, 128 - 2 * n), F32)], axis=1)
+    columns = [jnp.broadcast_to(gram[:, k : k + 1], (n, 128)) for k in range(n)]
     pivots = jnp.zeros((n, 128), F32)
+
+    def line(v, k):
+        return jnp.broadcast_to(v[k : k + 1, :], (n, 128))
+
     for k in range(n):
-        column = jnp.broadcast_to(t[:, k : k + 1], (n, 128))
-        pivot = jnp.broadcast_to(column[k : k + 1, :], (n, 128))
-        line = jnp.broadcast_to(t[k : k + 1, :], (n, 128))
+        pivot = line(columns[k], k)
         pivots = jnp.where(row == k, pivot, pivots)
-        t = t - where0(row > k, column / pivot) * line
+        if k == n - 1:
+            break
+        times = where0(row > k, columns[k]) * (1.0 / pivot)
+        for j in range(k + 1, n):
+            columns[j] = columns[j] - times * line(columns[k], j)
+        t = t - times * line(t, k)
     t = t / jnp.sqrt(pivots)
     upper = where0(row <= lane, t)[:, 0:n]
     return upper, t[:, n : 2 * n]
@@ -515,7 +555,7 @@
 
 def final_kernel(
     line_ref, a_hbm, hi_hbm, lo_hbm, out_hbm, proj_ref, tri_ref,
-    a, p_hi, p_lo, out, table, mp, in_sems, out_sems, *, cells,
+    a, p_hi, p_lo, out, table, mp, both, in_sems, out_sems, *, cells,
 ):
     gets = [
         pltpu.make_async_copy(src, dst, in_sems.at[i])
@@ -571,48 +611,58 @@
     none = jnp.zeros((M, M), F32)
     again = pair_dot((inv_one, none), gram, NN)
     again = pair_dot(again, (inv_one, none), NT)
+    right = (iota((K, KX), 1) // X == iota((K, KX), 0)).astype(F32)
+    wide = exact_dot(exact_dot(inv_one, proj, NT), right)
+    wide = jnp.concatenate([wide, inv_one], axis=1)
     upper_two, inv_two = factor(again[0] + again[1])
     tri_ref[...] = exact_dot(upper_two, upper_one)
-    mix = exact_dot(inv_two, inv_one)
-    mix_p = -exact_dot(mix, proj, NT)
-
-    rows = exact_dot((iota((MX, M), 0) // X == iota((MX, M), 1)).astype(F32), mix)
+    left = (iota((MX, M), 0) // X == iota((MX, M), 1)).astype(F32)
+    wide = exact_dot(exact_dot(left, inv_two), wide)
+    rows = wide[:, KX:]
     for j in range(M):
         table[j] = jnp.broadcast_to(rows[:, j : j + 1], (MX, 128))
     row, col = iota((MX, KX), 0), iota((MX, KX), 1)
-    n1, n2 = split2(where0(row % X == col % X, spread(mix_p, MX, KX)))
+    n1, n2 = split2(where0(row % X == col % X, -wide[:, 0:KX]))
     mp[...] = jnp.concatenate([n1, n2, n1], axis=1)
     for get in gets:
         get.wait()
 
-    def put(q):
-        at = pl.ds(2 * q, 2)
-        return pltpu.make_async_copy(out.at[:, at], out_hbm.at[:, at], out_sems.at[q])
+    def put(f):
+        return pltpu.make_async_copy(out.at[:, f], out_hbm.at[:, f], out_sems.at[f])
+
+    def basis_part(f):
+        p1 = p_hi[f]
+        return half_dot(mp[...], jnp.concatenate([p1, p1, p_lo[f]], axis=0))
+
+    def one(f, slot):
+        both[1 - slot] = basis_part(jnp.minimum(f + 1, F - 1))
+
+        halves = [slice(h * 128, (h + 1) * 128) for h in range(2)]
+        parts = [[a[j, f, :, half] for half in halves] for j in range(M)]
+        for k in range(M):
+            at = slice(k * X, (k + 1) * X)
+            totals = [both[slot, at, half] for half in halves]
+            for j in range(k + 1):
+                times = table[j, at, :]
+                totals = [total + times * part for total, part in zip(totals, parts[j])]
+            for half, total in zip(halves, totals):
+                out[k, f, :, half] = total
+        put(f).start()
+
+    both[0] = basis_part(0)
 
     def two(q, carry):
-        for i in range(2):
-            f = 2 * q + i
-            p1 = p_hi[f]
-            both = half_dot(mp[...], jnp.concatenate([p1, p1, p_lo[f]], axis=0))
-            for h in range(2):
-                half = slice(h * 128, (h + 1) * 128)
-                parts = [a[j, f, :, half] for j in range(M)]
-                for k in range(M):
-                    at = slice(k * X, (k + 1) * X)
-                    total = table[0, at, :] * parts[0]
-                    for j in range(1, k + 1):
-                        total = total + table[j, at, :] * parts[j]
-                    out[k, f, :, half] = total + both[at, half]
-        put(q).start()
+        one(2 * q, 0)
+        one(2 * q + 1, 1)
         return carry
 
     lax.fori_loop(0, TWO, two, 0)
 
-    def end(q, carry):
-        put(q).wait()
+    def end(f, carry):
+        put(f).wait()
         return carry
 
-    lax.fori_loop(0, TWO, end, 0)
+    lax.fori_loop(0, F, end, 0)
 
 
 def final(lines, a, p_hi, p_lo, cells):
@@ -634,8 +684,9 @@
             pltpu.VMEM((M, F, X, Y), F32),
             pltpu.VMEM((M, MX, 128), F32),
             pltpu.VMEM((MX, 3 * KX), BF16),
+            pltpu.VMEM((2, MX, Y), F32),
             pltpu.SemaphoreType.DMA((3,)),
-            pltpu.SemaphoreType.DMA((TWO,)),
+            pltpu.SemaphoreType.DMA((F,)),
         ],
         name="final",
     )(lines, a, p_hi, p_lo)
@@ -656,17 +707,16 @@
 
     before = lax.ppermute(last, GX, onward(GX))
     after = lax.ppermute(first, GX, back(GX))
-    applied, yfirst, ylast, weights = inside(
+    applied, yfirst, ylast, weights, wy = inside(
         krylov_block, flux_along, flux_across, collision, wall_mask, wall_type, field_rates,
         wall_table,
     )
     ybefore = lax.ppermute(ylast, GY, onward(GY))
     yafter = lax.ppermute(yfirst, GY, back(GY))
     gp, p_hi, p_lo = basis(prior_basis)
-    cb, ca = columns(ybefore, yafter, flux_across)
     sizes = [lax.axis_size(stage) for stage in STAGES]
     applied, lines = with_halo(
-        applied, p_hi, p_lo, before, after, cb, ca, weights, gp, sizes[0]
+        applied, p_hi, p_lo, before, after, ybefore, yafter, weights, wy, gp, sizes[0]
     )
     lines = middle(sent_to_all(lines, STAGES[0]), sizes[1])
     lines = sent_to_all(lines, STAGES[1])

time: 109 us -> 93 us (0.85)
  Pallas kernels: 58.6 us -> 44.3 us
  local copies, waits for them, and re-layouts: 2.51 us -> 1.29 us
    pallas_call x3 -> x2, Pallas kernels: 20 us -> 13.4 us  [the longest x1 10.5 us: with_halo(): pl.pallas_call(halo_kernel, in_specs=[anywhere] * 5 + [vmem] * 5, out_spe...]
    pallas_call x1, Pallas kernels: 16.1 us -> 12.7 us  [final(): pl.pallas_call(functools.partial(final_kernel, cells=cells), in_specs=[vm...]
    pallas_call x1, Pallas kernels: 13.2 us -> 9.85 us  [inside(): pl.pallas_call(functools.partial(inside_kernel, step_m=step_m), grid=(M /...]
    unnamed x8, local copies, waits for them, and re-layouts: 2.51 us -> 1.29 us
  transfers between devices with their start and end apart: 4 -> 4, of which waited for: 0 -> 0; matrix products, arithmetic and copies ran while one was open for 0% -> 0% of each run, Pallas kernels for 22% -> 18%
where the time goes in v2:
time: 93 us; the launch traced here: 92.5 us
  Pallas kernels  44.3 us (48%)
  blocking collectives  35 us (38%)
  starting transfers between devices  11.2 us (12%)
  local copies, waits for them, and re-layouts  1.29 us (1%)
    all_to_all x2, blocking collectives, sent_to_all(): return lax.all_to_all(copies, axis, split_axis=0, concat_axis=0, tiled=True)  35 us
    pallas_call x1, Pallas kernels, final(): pl.pallas_call(functools.partial(final_kernel, cells=cells), in_specs=[vm...  12.7 us
    pallas_call x1, Pallas kernels, with_halo(): pl.pallas_call(halo_kernel, in_specs=[anywhere] * 5 + [vmem] * 5, out_spe...  10.5 us
    pallas_call x1, Pallas kernels, inside(): pl.pallas_call(functools.partial(inside_kernel, step_m=step_m), grid=(M /...  9.85 us
    pallas_call x1, Pallas kernels, basis(): pl.pallas_call(basis_kernel, in_specs=[anywhere], out_specs=[pl.BlockSpec...  6.74 us
    ppermute x1, starting transfers between devices, on_device(): ybefore = lax.ppermute(ylast, GY, onward(GY))  4.04 us
    ppermute x1, starting transfers between devices, on_device(): before = lax.ppermute(last, GX, onward(GX))  3.99 us
    pallas_call x1, Pallas kernels, pack(): pl.pallas_call(pack_kernel, in_specs=[anywhere], out_specs=[anywhere] * 2...  2.86 us
  transfers between devices with their start and end apart: 4, of which 0 were waited for; matrix products, arithmetic and copies ran while one was open for 0% of the time, Pallas kernels for 18%

profile of v2, /device:TPU:1, one launch (start us, length us, event | category | flops | bytes accessed | tf_op | source)
XLA Modules:
  0.0 92.5 jit_solution(16652506195452019337)
XLA Ops:
  0.6 2.9 %pack.1 = (f32[8,104,256]{2,1,0:T(8,128)}, f32[8,104,256]{2,1,0:T(8,128)}) custom-call(f32[16,26,8,256]{3,2,1,0:T(8,128)} %v_hbm.1), custom_call_target="tpu_custom_call" | custom-call | flops 1000000 | bytes 6000000 | tf_op jit(solution)/shard_map/pack/pallas_call | solution.py:126
  3.5 4.0 %collective-permute-start = (f32[8,104,256]{2,1,0:T(8,128)}, f32[8,104,256]{2,1,0:T(8,128)S(1)}, u32[]{:S(2)}, u32[]{:S(2)}) collective-permute-start(f32[8,104,256]{2,1,0:T(8,128)} %get-tuple-element.21), channel_id=1, source_target_pairs={{0,8},{8,16},{16,24},{24,32},{32,40},{40,48},{48,56},{56,64},{64,7... | collective-permute-start | bytes 2555912 | tf_op jit(solution)/shard_map/ppermute | solution.py:708
  7.5 1.3 %collective-permute-start.1 = (f32[8,104,256]{2,1,0:T(8,128)}, f32[8,104,256]{2,1,0:T(8,128)S(1)}, u32[]{:S(2)}, u32[]{:S(2)}) collective-permute-start(f32[8,104,256]{2,1,0:T(8,128)} %get-tuple-element.22), channel_id=1, source_target_pairs={{8,0},{16,8},{24,16},{32,24},{40,32},{48,40},{56,48},{64,56},{72,6... | collective-permute-start | bytes 2555912 | tf_op jit(solution)/shard_map/ppermute | solution.py:709
  8.8 9.8 %inside.1 = (f32[16,26,8,256]{3,2,1,0:T(8,128)}, f32[208,128]{1,0:T(8,128)}, f32[208,128]{1,0:T(8,128)}, bf16[2,208,208]{2,1,0:T(8,128)(2,1)}, bf16[2,208,208]{2,1,0:T(8,128)(2,1)}) custom-call(f32[16,26,8,256]{3,2,1,0:T(8,128)} %v_hbm.1, f32[26,26]{1,0:T(8,128)} %along_ref.1, f32[26,26]{1,0:T(8,128)} %across_ref.1, f32[8,256]{1,0:T(8,128)} %coll_ref.1, ...), custom_call_target="tpu_custom_call" | custom-call | flops 8000000000 | bytes 7000000 | tf_op jit(solution)/shard_map/inside/pallas_call | solution.py:224
  18.6 4.0 %collective-permute-start.2 = (f32[208,128]{1,0:T(8,128)}, f32[208,128]{1,0:T(8,128)S(1)}, u32[]{:S(2)}, u32[]{:S(2)}) collective-permute-start(f32[208,128]{1,0:T(8,128)} %get-tuple-element.23), channel_id=1, source_target_pairs={{0,1},{1,2},{2,3},{3,4},{4,5},{5,6},{6,7},{8,9},{9,10},{10,11},{11... | collective-permute-start | bytes 319496 | tf_op jit(solution)/shard_map/ppermute | solution.py:714
  22.7 1.9 %collective-permute-start.3 = (f32[208,128]{1,0:T(8,128)}, f32[208,128]{1,0:T(8,128)S(1)}, u32[]{:S(2)}, u32[]{:S(2)}) collective-permute-start(f32[208,128]{1,0:T(8,128)} %get-tuple-element.24), channel_id=1, source_target_pairs={{1,0},{2,1},{3,2},{4,3},{5,4},{6,5},{7,6},{9,8},{10,9},{11,10},{12... | collective-permute-start | bytes 319496 | tf_op jit(solution)/shard_map/ppermute | solution.py:715
  24.6 6.7 %basis.1 = (f32[16,128]{1,0:T(8,128)}, bf16[26,192,256]{2,1,0:T(8,128)(2,1)}, bf16[26,192,256]{2,1,0:T(8,128)(2,1)}) custom-call(f32[24,26,8,256]{3,2,1,0:T(8,128)} %p_hbm.1), custom_call_target="tpu_custom_call" | custom-call | flops 8000000000 | bytes 10000000 | tf_op jit(solution)/shard_map/basis/pallas_call | solution.py:328
  31.4 0.0 collective-permute-done.2.yb_ref
  31.4 0.0 copy-start.2
  31.4 0.0 collective-permute-done.3.ya_ref
  31.4 0.0 copy-start.3
  31.4 0.0 collective-permute-done.before_hbm
  31.4 0.0 copy-start
  31.4 0.0 collective-permute-done.1.after_hbm
  31.4 0.0 copy-start.1
  31.4 0.6 copy-done.2
  32.0 0.1 copy-done.3
  32.1 0.4 copy-done
  32.5 0.2 copy-done.1
  32.7 10.5 %halo.1 = (f32[16,26,8,256]{3,2,1,0:T(8,128)}, f32[16,16,128]{2,1,0:T(8,128)}) custom-call(f32[16,26,8,256]{3,2,1,0:T(8,128)} %get-tuple-element.18.a_hbm, bf16[26,192,256]{2,1,0:T(8,128)(2,1)} %get-tuple-element.19.hi_hbm, bf16[26,192,256]{2,1,0:T(8,128)(2,1)} %get-tuple-element.20.lo_hbm, f32[8,104,256]{2,1,0:T(8,128)} %copy-done, ...), custom_call_target="tpu_custom_call" | custom-call | flops 8000000000 | bytes 14000000 | tf_op jit(solution)/shard_map/halo/pallas_call | solution.py:445
  43.3 14.4 %all_to_all.10.in_ref = f32[16,16,128]{2,1,0:T(8,128)} all-to-all(f32[16,16,128]{2,1,0:T(8,128)} %get-tuple-element.28), channel_id=1, replica_groups=mesh['gx_z'=8,'gx_x'=4,'gy_y'=4,'gy_c'=2] {'gx_x','gy_y'}, dimensions={0} | all-to-all | bytes 262144 | tf_op jit(solution)/shard_map/all_to_all | solution.py:499
  57.6 1.6 %middle.1 = f32[16,16,128]{2,1,0:T(8,128)} custom-call(f32[16,16,128]{2,1,0:T(8,128)} %all_to_all.10.in_ref), custom_call_target="tpu_custom_call" | custom-call | tf_op jit(solution)/shard_map/middle/pallas_call | solution.py:491
  59.2 20.6 %all_to_all.11.line_ref = f32[16,16,128]{2,1,0:T(8,128)} all-to-all(f32[16,16,128]{2,1,0:T(8,128)} %middle.1), channel_id=1, replica_groups=mesh['gx_z'=8,'gx_x'=4,'gy_y'=4,'gy_c'=2] {'gx_z','gy_c'}, dimensions={0} | all-to-all | bytes 262144 | tf_op jit(solution)/shard_map/all_to_all | solution.py:499
  79.8 12.7 %final.1 = (f32[16,26,8,256]{3,2,1,0:T(8,128)}, f32[16,24]{1,0:T(8,128)}, f32[16,16]{1,0:T(8,128)}) custom-call(f32[16,16,128]{2,1,0:T(8,128)} %all_to_all.11.line_ref, f32[16,26,8,256]{3,2,1,0:T(8,128)} %get-tuple-element.29.a_hbm, bf16[26,192,256]{2,1,0:T(8,128)(2,1)} %get-tuple-element.19.hi_hbm, bf16[26,192,256]{2,1,0:T(8,128)(2,1)} %get-tuple-element.20.lo_hbm), custom_call_target="tpu_custom_call" | custom-call | tf_op jit(solution)/shard_map/final/pallas_call | solution.py:671
Async XLA Ops:
  3.5 27.9 %collective-permute-start = (f32[8,104,256]{2,1,0:T(8,128)}, f32[8,104,256]{2,1,0:T(8,128)S(1)}, u32[]{:S(2)}, u32[]{:S(2)}) collective-permute-start(f32[8,104,256]{2,1,0:T(8,128)} %get-tuple-element.21), channel_id=1, source_target_pairs={{0,8},{8,16},{16,24},{24,32},{32,40},{40,48},{48,56},{56,64},{64,7... | collective-permute-start | bytes 2555912 | tf_op jit(solution)/shard_map/ppermute | solution.py:708
  7.5 23.9 %collective-permute-start.1 = (f32[8,104,256]{2,1,0:T(8,128)}, f32[8,104,256]{2,1,0:T(8,128)S(1)}, u32[]{:S(2)}, u32[]{:S(2)}) collective-permute-start(f32[8,104,256]{2,1,0:T(8,128)} %get-tuple-element.22), channel_id=1, source_target_pairs={{8,0},{16,8},{24,16},{32,24},{40,32},{48,40},{56,48},{64,56},{72,6... | collective-permute-start | bytes 2555912 | tf_op jit(solution)/shard_map/ppermute | solution.py:709
  18.6 12.7 %collective-permute-start.2 = (f32[208,128]{1,0:T(8,128)}, f32[208,128]{1,0:T(8,128)S(1)}, u32[]{:S(2)}, u32[]{:S(2)}) collective-permute-start(f32[208,128]{1,0:T(8,128)} %get-tuple-element.23), channel_id=1, source_target_pairs={{0,1},{1,2},{2,3},{3,4},{4,5},{5,6},{6,7},{8,9},{9,10},{10,11},{11... | collective-permute-start | bytes 319496 | tf_op jit(solution)/shard_map/ppermute | solution.py:714
  22.7 8.7 %collective-permute-start.3 = (f32[208,128]{1,0:T(8,128)}, f32[208,128]{1,0:T(8,128)S(1)}, u32[]{:S(2)}, u32[]{:S(2)}) collective-permute-start(f32[208,128]{1,0:T(8,128)} %get-tuple-element.24), channel_id=1, source_target_pairs={{1,0},{2,1},{3,2},{4,3},{5,4},{6,5},{7,6},{9,8},{10,9},{11,10},{12... | collective-permute-start | bytes 319496 | tf_op jit(solution)/shard_map/ppermute | solution.py:715
  31.4 0.6 copy-start.2
  31.4 0.7 copy-start.3
  31.4 1.1 %copy-start = (f32[8,104,256]{2,1,0:T(8,128)}, f32[8,104,256]{2,1,0:T(8,128)S(1)}, u32[]{:S(2)}) copy-start(f32[8,104,256]{2,1,0:T(8,128)S(1)} %collective-permute-done.before_hbm) | copy-start | bytes 2555908
  31.4 1.3 %copy-start.1 = (f32[8,104,256]{2,1,0:T(8,128)}, f32[8,104,256]{2,1,0:T(8,128)S(1)}, u32[]{:S(2)}) copy-start(f32[8,104,256]{2,1,0:T(8,128)S(1)} %collective-permute-done.1.after_hbm) | copy-start | bytes 2555908

commit v3 on v2

--- a/solution.py
+++ b/solution.py
@@ -26,6 +26,7 @@
 MX = M * X
 KX = K * X
 PAIRS = M // 2
+LIMIT = 32 * 2**20
 HALO = 4 * F
 
 NN = (((1,), (0,)), ((), ()))
@@ -51,6 +52,14 @@
     rest = v - hi.astype(F32)
     mid = rest.astype(BF16)
     return hi, mid, (rest - mid.astype(F32)).astype(BF16)
+
+
+def kept(*shape_and_type):
+    return pltpu.VMEM(*shape_and_type)
+
+
+def near(v):
+    return pltpu.with_memory_space_constraint(v, pltpu.VMEM)
 
 
 def iota(shape, dim):
@@ -90,61 +99,36 @@
     return jnp.concatenate([left, right], axis=1)
 
 
-def pack_kernel(v_hbm, first_hbm, last_hbm, v, first, last, sems):
-    def get(q):
-        at = pl.ds(2 * q, 2)
-        return pltpu.make_async_copy(v_hbm.at[at], v.at[at], sems.at[0, q])
-
-    def puts(q):
-        return (
-            pltpu.make_async_copy(first.at[q], first_hbm.at[q], sems.at[1, q]),
-            pltpu.make_async_copy(last.at[q], last_hbm.at[q], sems.at[2, q]),
-        )
-
-    for q in range(PAIRS):
-        get(q).start()
-
+def pack_kernel(v, first, last):
     def pair(q, carry):
-        get(q).wait()
         for i in range(2):
             for f in range(F):
                 at = (i * F + f) * 2
                 first[q, at : at + 2, :] = v[2 * q + i, f, 0:2, :]
                 last[q, at : at + 2, :] = v[2 * q + i, f, X - 2 : X, :]
-        for put in puts(q):
-            put.start()
         return carry
 
     lax.fori_loop(0, PAIRS, pair, 0)
-    for q in range(PAIRS):
-        for put in puts(q):
-            put.wait()
 
 
 def pack(v):
-    anywhere = pl.BlockSpec(memory_space=pl.ANY)
+    vmem = pl.BlockSpec(memory_space=pltpu.VMEM)
     return pl.pallas_call(
         pack_kernel,
-        in_specs=[anywhere],
-        out_specs=[anywhere] * 2,
-        out_shape=[jax.ShapeDtypeStruct((PAIRS, HALO, Y), F32)] * 2,
-        scratch_shapes=[
-            pltpu.VMEM((M, F, X, Y), F32),
-            pltpu.VMEM((PAIRS, HALO, Y), F32),
-            pltpu.VMEM((PAIRS, HALO, Y), F32),
-            pltpu.SemaphoreType.DMA((3, PAIRS)),
-        ],
+        in_specs=[vmem],
+        out_specs=[vmem] * 2,
+        out_shape=[kept((PAIRS, HALO, Y), F32)] * 2,
+        compiler_params=pltpu.CompilerParams(vmem_limit_bytes=LIMIT),
         cost_estimate=pl.CostEstimate(flops=10**6, bytes_accessed=6 * 10**6, transcendentals=0),
         name="pack",
-    )(v)
+    )(near(v))
 
 
 def inside_kernel(
     v_ref, along_ref, across_ref, coll_ref, mask_ref, type_ref, rate_ref, table_ref,
-    out_ref, yfirst_ref, ylast_ref, halo_ref, ycol_ref, w, coeff, *, step_m,
+    out_ref, yfirst_ref, ylast_ref, halo_ref, ycol_ref, w, coeff, both,
 ):
-    @pl.when(pl.program_id(0) == 0)
-    def _():
+    if True:
         eye = (iota((F, F), 0) == iota((F, F), 1)).astype(F32)
         along, across = 0.5 * along_ref[...], 0.5 * across_ref[...]
         plus, minus = along - 4.0 * DAMP * eye, -along - 4.0 * DAMP * eye
@@ -194,66 +178,59 @@
 
     lane2 = iota((FX, 128), 1) // 2
 
-    def one(i):
-        m = pl.program_id(0) * step_m + i
-        v = v_ref[i].reshape(FX, Y)
+    def product(m):
+        hi, lo = split2(v_ref[m].reshape(FX, Y))
+        return half_dot(w[...], jnp.concatenate([hi, hi, lo], axis=0))
+
+    def one(m, slot):
+        both[1 - slot] = product(jnp.minimum(m + 1, M - 1))
+        v = v_ref[m].reshape(FX, Y)
         mine = lane2 == m
         yfirst_ref[...] = jnp.where(mine, roll(v[:, 0:128], 2 * m, 1), yfirst_ref[...])
         ylast_ref[...] = jnp.where(mine, roll(v[:, Y - 128 :], 2 * m + 2, 1), ylast_ref[...])
-        hi, lo = split2(v)
-        both = half_dot(w[...], jnp.concatenate([hi, hi, lo], axis=0))
-        u = both[FX:]
-        out = both[:FX] + coeff[...] * v
+        u = both[slot, FX:]
+        out = both[slot, :FX] + coeff[...] * v
         side = 4.0 * DAMP * v
         two = DAMP * v
         out = out + moved(u - side, -1) - moved(u + side, 1)
         out = out + moved(two, -2) + moved(two, 2)
-        out_ref[i] = out.reshape(F, X, Y)
+        out_ref[m] = out.reshape(F, X, Y)
+
+    both[0] = product(0)
 
     def couple(i, carry):
-        one(2 * i)
-        one(2 * i + 1)
+        one(2 * i, 0)
+        one(2 * i + 1, 1)
         return carry
 
-    lax.fori_loop(0, step_m // 2, couple, 0)
-
-
-def inside(v, along, across, coll, mask, types, rates, table, step_m=4):
+    lax.fori_loop(0, M // 2, couple, 0)
+
+
+def inside(v, along, across, coll, mask, types, rates, table):
     smem = pl.BlockSpec(memory_space=pltpu.SMEM)
-    whole2 = lambda i: (0, 0)
+    vmem = pl.BlockSpec(memory_space=pltpu.VMEM)
     return pl.pallas_call(
-        functools.partial(inside_kernel, step_m=step_m),
-        grid=(M // step_m,),
-        in_specs=[
-            pl.BlockSpec((step_m, F, X, Y), lambda i: (i, 0, 0, 0)),
-            pl.BlockSpec((F, F), whole2),
-            pl.BlockSpec((F, F), whole2),
-            pl.BlockSpec((X, Y), whole2),
-            pl.BlockSpec((X, Y), whole2),
-            pl.BlockSpec((X, Y), whole2),
-            smem,
-            smem,
+        inside_kernel,
+        in_specs=[vmem] * 6 + [smem] * 2,
+        out_specs=[vmem] * 5,
+        out_shape=[
+            kept((M, F, X, Y), F32),
+            kept((FX, 128), F32),
+            kept((FX, 128), F32),
+            kept((2, FX, 2 * HALO), BF16),
+            kept((2, FX, FX), BF16),
         ],
-        out_specs=[
-            pl.BlockSpec((step_m, F, X, Y), lambda i: (i, 0, 0, 0)),
-            pl.BlockSpec((FX, 128), whole2),
-            pl.BlockSpec((FX, 128), whole2),
-            pl.BlockSpec((2, FX, 2 * HALO), lambda i: (0, 0, 0)),
-            pl.BlockSpec((2, FX, FX), lambda i: (0, 0, 0)),
+        scratch_shapes=[
+            pltpu.VMEM((2 * FX, 3 * FX), BF16),
+            pltpu.VMEM((FX, Y), F32),
+            pltpu.VMEM((2, 2 * FX, Y), F32),
         ],
-        out_shape=[
-            jax.ShapeDtypeStruct((M, F, X, Y), F32),
-            jax.ShapeDtypeStruct((FX, 128), F32),
-            jax.ShapeDtypeStruct((FX, 128), F32),
-            jax.ShapeDtypeStruct((2, FX, 2 * HALO), BF16),
-            jax.ShapeDtypeStruct((2, FX, FX), BF16),
-        ],
-        scratch_shapes=[pltpu.VMEM((2 * FX, 3 * FX), BF16), pltpu.VMEM((FX, Y), F32)],
+        compiler_params=pltpu.CompilerParams(vmem_limit_bytes=LIMIT),
         cost_estimate=pl.CostEstimate(
             flops=8 * 10**9, bytes_accessed=7 * 10**6, transcendentals=0
         ),
         name="inside",
-    )(v, along, across, coll, mask, types, rates, table)
+    )(near(v), along, across, coll, mask, types, rates, table)
 
 
 def diagonal(big, small, left, right):
@@ -271,19 +248,7 @@
 TWO = F // 2
 
 
-def basis_kernel(p_hbm, out_ref, hi_hbm, lo_hbm, p, hi_ref, lo_ref, big_ref, small_ref, in_sem, out_sem):
-    def get(f):
-        return pltpu.make_async_copy(p_hbm.at[:, f], p.at[:, f], in_sem.at[f])
-
-    def puts(q):
-        at = pl.ds(TWO * q, TWO)
-        return (
-            pltpu.make_async_copy(hi_ref.at[at], hi_hbm.at[at], out_sem.at[0, q]),
-            pltpu.make_async_copy(lo_ref.at[at], lo_hbm.at[at], out_sem.at[1, q]),
-        )
-
-    for f in range(F):
-        get(f).start()
+def basis_kernel(p, out_ref, hi_ref, lo_ref, big_ref, small_ref):
     big_ref[...] = jnp.zeros_like(big_ref)
     small_ref[...] = jnp.zeros_like(small_ref)
 
@@ -291,14 +256,11 @@
         his, los = [], []
         for i in range(TWO):
             f = q * TWO + i
-            get(f).wait()
             hi, lo = split2(p[:, f].reshape(KX, Y))
             hi_ref[f] = hi
             lo_ref[f] = lo
             his.append(hi)
             los.append(lo)
-        for put in puts(q):
-            put.start()
         half = [lo * jnp.asarray(0.5, BF16) for lo in los]
         big_ref[...] += half_dot(jnp.concatenate(his, axis=1), jnp.concatenate(his, axis=1), NT)
         small_ref[...] += half_dot(
@@ -318,61 +280,27 @@
         line = line + where0(lane >= 120, roll(part[16:24], 104, 1))
         out_ref[8 * half : 8 * half + 8, :] = line
 
-    for q in range(2):
-        for put in puts(q):
-            put.wait()
-
 
 def basis(p):
-    anywhere = pl.BlockSpec(memory_space=pl.ANY)
+    vmem = pl.BlockSpec(memory_space=pltpu.VMEM)
     return pl.pallas_call(
         basis_kernel,
-        in_specs=[anywhere],
-        out_specs=[pl.BlockSpec(memory_space=pltpu.VMEM), anywhere, anywhere],
-        out_shape=[
-            jax.ShapeDtypeStruct((16, 128), F32),
-            jax.ShapeDtypeStruct((F, KX, Y), BF16),
-            jax.ShapeDtypeStruct((F, KX, Y), BF16),
-        ],
-        scratch_shapes=[
-            pltpu.VMEM((K, F, X, Y), F32),
-            pltpu.VMEM((F, KX, Y), BF16),
-            pltpu.VMEM((F, KX, Y), BF16),
-            pltpu.VMEM((KX, KX), F32),
-            pltpu.VMEM((KX, KX), F32),
-            pltpu.SemaphoreType.DMA((F,)),
-            pltpu.SemaphoreType.DMA((2, 2)),
-        ],
+        in_specs=[vmem],
+        out_specs=[vmem] * 3,
+        out_shape=[kept((16, 128), F32), kept((F, KX, Y), BF16), kept((F, KX, Y), BF16)],
+        scratch_shapes=[pltpu.VMEM((KX, KX), F32), pltpu.VMEM((KX, KX), F32)],
+        compiler_params=pltpu.CompilerParams(vmem_limit_bytes=LIMIT),
         cost_estimate=pl.CostEstimate(
             flops=8 * 10**9, bytes_accessed=10 * 10**6, transcendentals=0
         ),
         name="basis",
-    )(p)
+    )(near(p))
 
 
 def halo_kernel(
-    a_hbm, hi_hbm, lo_hbm, before_hbm, after_hbm, yb_ref, ya_ref, w_ref, wy_ref, gp_ref,
-    out_hbm, line_ref, a, p_hi, p_lo, before, after, edge, acc, a_sem, sems,
+    inner, p_hi, p_lo, before, after, yb_ref, ya_ref, w_ref, wy_ref, gp_ref,
+    a, line_ref, edge, acc,
 ):
-    def get(q):
-        at = pl.ds(2 * q, 2)
-        return (
-            pltpu.make_async_copy(a_hbm.at[at], a.at[at], a_sem.at[0, q]),
-            pltpu.make_async_copy(before_hbm.at[q], before.at[q], a_sem.at[1, q]),
-            pltpu.make_async_copy(after_hbm.at[q], after.at[q], a_sem.at[2, q]),
-        )
-
-    def put(q):
-        at = pl.ds(2 * q, 2)
-        return pltpu.make_async_copy(a.at[at], out_hbm.at[at], a_sem.at[3, q])
-
-    get_hi = pltpu.make_async_copy(hi_hbm, p_hi, sems.at[0])
-    get_lo = pltpu.make_async_copy(lo_hbm, p_lo, sems.at[1])
-    for q in range(PAIRS):
-        for each in get(q):
-            each.start()
-    get_hi.start()
-    get_lo.start()
     lane = iota((FX, 128), 1)
     yb, ya = yb_ref[...], ya_ref[...]
     hi, lo = split2(jnp.concatenate([yb, ya], axis=1))
@@ -383,8 +311,6 @@
     edge[1] = DAMP * ya + where0(lane % 2 == 1, roll(term, 1, 1))
 
     def pair(q):
-        for each in get(q):
-            each.wait()
         for i in range(2):
             m = 2 * q + i
             mine = slice(i * 2 * F, (i + 1) * 2 * F)
@@ -393,10 +319,9 @@
             h = jnp.concatenate([hi, h - hi], axis=0).astype(BF16)
             left = where0(lane < 2, roll(edge[0], (128 - 2 * m) % 128, 1))
             right = where0(lane >= 126, roll(edge[1], 126 - 2 * m, 1))
-            part = a[m].reshape(FX, Y) + jnp.concatenate([left, right], axis=1)
+            part = inner[m].reshape(FX, Y) + jnp.concatenate([left, right], axis=1)
             part = part + (half_dot(w_ref[0], h) + half_dot(w_ref[1], h))
             a[m] = part.reshape(F, X, Y)
-        put(q).start()
 
     def pairs(q, carry):
         pair(2 * q)
@@ -405,9 +330,6 @@
 
     lax.fori_loop(0, PAIRS // 2, pairs, 0)
     acc[...] = jnp.zeros_like(acc)
-    get_hi.wait()
-    get_lo.wait()
-
     def some(q, carry):
         rows, cols = [], []
         for i in range(TWO):
@@ -432,40 +354,28 @@
         for copy in range(line_ref.shape[0]):
             line_ref[copy, 8 * half : 8 * half + 8, :] = line
 
-    def end(q, carry):
-        put(q).wait()
-        return carry
-
-    lax.fori_loop(0, PAIRS, end, 0)
-
 
 def with_halo(a, p_hi, p_lo, before, after, yb, ya, weights, wy, gp, copies):
     vmem = pl.BlockSpec(memory_space=pltpu.VMEM)
-    anywhere = pl.BlockSpec(memory_space=pl.ANY)
     return pl.pallas_call(
         halo_kernel,
-        in_specs=[anywhere] * 5 + [vmem] * 5,
-        out_specs=[anywhere, vmem],
-        out_shape=[
-            jax.ShapeDtypeStruct((M, F, X, Y), F32),
-            jax.ShapeDtypeStruct((copies, 16, 128), F32),
-        ],
+        in_specs=[vmem] * 10,
+        out_specs=[vmem, vmem],
+        out_shape=[kept((M, F, X, Y), F32), kept((copies, 16, 128), F32)],
         scratch_shapes=[
-            pltpu.VMEM((M, F, X, Y), F32),
-            pltpu.VMEM((F, KX, Y), BF16),
-            pltpu.VMEM((F, KX, Y), BF16),
-            pltpu.VMEM((PAIRS, HALO, Y), F32),
-            pltpu.VMEM((PAIRS, HALO, Y), F32),
             pltpu.VMEM((2, FX, 128), F32),
             pltpu.VMEM((2 * (KX + MX), 2 * MX), F32),
-            pltpu.SemaphoreType.DMA((4, PAIRS)),
-            pltpu.SemaphoreType.DMA((2,)),
         ],
+        input_output_aliases={0: 0},
+        compiler_params=pltpu.CompilerParams(vmem_limit_bytes=LIMIT),
         cost_estimate=pl.CostEstimate(
             flops=8 * 10**9, bytes_accessed=14 * 10**6, transcendentals=0
         ),
         name="halo",
-    )(a, p_hi, p_lo, before, after, yb, ya, weights, wy, gp)
+    )(
+        near(a), near(p_hi), near(p_lo), near(before), near(after), near(yb), near(ya), weights,
+        wy, gp,
+    )
 
 
 def pair_total(ref):
@@ -490,9 +400,10 @@
 def middle(lines, copies):
     return pl.pallas_call(
         middle_kernel,
-        out_shape=jax.ShapeDtypeStruct((copies, 16, 128), F32),
+        out_shape=kept((copies, 16, 128), F32),
+        compiler_params=pltpu.CompilerParams(vmem_limit_bytes=LIMIT),
         name="middle",
-    )(lines)
+    )(near(lines))
 
 
 def sent_to_all(copies, axis):
@@ -554,16 +465,9 @@
 
 
 def final_kernel(
-    line_ref, a_hbm, hi_hbm, lo_hbm, out_hbm, proj_ref, tri_ref,
-    a, p_hi, p_lo, out, table, mp, both, in_sems, out_sems, *, cells,
+    line_ref, a, p_hi, p_lo, out_hbm, proj_ref, tri_ref,
+    out, table, mp, both, out_sems, *, cells,
 ):
-    gets = [
-        pltpu.make_async_copy(src, dst, in_sems.at[i])
-        for i, (src, dst) in enumerate(((a_hbm, a), (hi_hbm, p_hi), (lo_hbm, p_lo)))
-    ]
-    for get in gets:
-        get.start()
-
     hi, lo = pair_total(line_ref)
     hi, lo = two_sum(hi, lo)
     odd = cells
@@ -624,9 +528,6 @@
     row, col = iota((MX, KX), 0), iota((MX, KX), 1)
     n1, n2 = split2(where0(row % X == col % X, -wide[:, 0:KX]))
     mp[...] = jnp.concatenate([n1, n2, n1], axis=1)
-    for get in gets:
-        get.wait()
-
     def put(f):
         return pltpu.make_async_copy(out.at[:, f], out_hbm.at[:, f], out_sems.at[f])
 
@@ -670,7 +571,7 @@
     anywhere = pl.BlockSpec(memory_space=pl.ANY)
     return pl.pallas_call(
         functools.partial(final_kernel, cells=cells),
-        in_specs=[vmem, anywhere, anywhere, anywhere],
+        in_specs=[vmem] * 4,
         out_specs=[anywhere, vmem, vmem],
         out_shape=[
             jax.ShapeDtypeStruct((M, F, X, Y), F32),
@@ -679,17 +580,14 @@
         ],
         scratch_shapes=[
             pltpu.VMEM((M, F, X, Y), F32),
-            pltpu.VMEM((F, KX, Y), BF16),
-            pltpu.VMEM((F, KX, Y), BF16),
-            pltpu.VMEM((M, F, X, Y), F32),
             pltpu.VMEM((M, MX, 128), F32),
             pltpu.VMEM((MX, 3 * KX), BF16),
             pltpu.VMEM((2, MX, Y), F32),
-            pltpu.SemaphoreType.DMA((3,)),
             pltpu.SemaphoreType.DMA((F,)),
         ],
+        compiler_params=pltpu.CompilerParams(vmem_limit_bytes=LIMIT),
         name="final",
-    )(lines, a, p_hi, p_lo)
+    )(near(lines), near(a), near(p_hi), near(p_lo))
 
 
 def on_device(

time: 93 us -> 79.6 us (0.86)
  Pallas kernels: 44.3 us -> 26.4 us
  waiting for transfers between devices: 0.01 us -> 2.9 us
    pallas_call x5, Pallas kernels: 31.6 us -> 17.3 us  [the longest x1 7.37 us: inside(): pl.pallas_call(inside_kernel, in_specs=[vmem] * 6 + [smem] * 2, out_specs...]
    pallas_call x1, Pallas kernels: 12.7 us -> 9.13 us  [final(): pl.pallas_call(functools.partial(final_kernel, cells=cells), in_specs=[vm...]
    ppermute x1, waiting for transfers between devices: 0.01 us -> 2.32 us  [on_device(): after = lax.ppermute(first, GX, back(GX))]
    unnamed x8 -> x20, local copies, waits for them, and re-layouts: 1.29 us -> 2 us
  transfers between devices with their start and end apart: 4 -> 4, of which waited for: 0 -> 2; matrix products, arithmetic and copies ran while one was open for 0% -> 0% of each run, Pallas kernels for 18% -> 14%
where the time goes in v3:
time: 79.6 us; the launch traced here: 79.3 us
  blocking collectives  35.6 us (45%)
  Pallas kernels  26.4 us (33%)
  starting transfers between devices  11.5 us (14%)
  waiting for transfers between devices  2.9 us (4%)
  local copies, waits for them, and re-layouts  2 us (3%)
  between operations  0.82 us (1%)
    all_to_all x2, blocking collectives, sent_to_all(): return lax.all_to_all(copies, axis, split_axis=0, concat_axis=0, tiled=True)  35.6 us
    pallas_call x1, Pallas kernels, final(): pl.pallas_call(functools.partial(final_kernel, cells=cells), in_specs=[vm...  9.13 us
    pallas_call x1, Pallas kernels, inside(): pl.pallas_call(inside_kernel, in_specs=[vmem] * 6 + [smem] * 2, out_specs...  7.37 us
    pallas_call x1, Pallas kernels, with_halo(): pl.pallas_call(halo_kernel, in_specs=[vmem] * 10, out_specs=[vmem, vmem],...  5.35 us
    ppermute x1, starting transfers between devices, on_device(): ybefore = lax.ppermute(ylast, GY, onward(GY))  4.04 us
    ppermute x1, starting transfers between devices, on_device(): before = lax.ppermute(last, GX, onward(GX))  3.99 us
    pallas_call x1, Pallas kernels, basis(): pl.pallas_call(basis_kernel, in_specs=[vmem], out_specs=[vmem] * 3, out_s...  3.78 us
    ppermute x1, waiting for transfers between devices, on_device(): after = lax.ppermute(first, GX, back(GX))  2.32 us
  transfers between devices with their start and end apart: 4, of which 2 were waited for; matrix products, arithmetic and copies ran while one was open for 0% of the time, Pallas kernels for 14%

profile of v3, /device:TPU:1, one launch (start us, length us, event | category | flops | bytes accessed | tf_op | source)
XLA Modules:
  0.0 79.3 jit_solution(18419179974050029472)
XLA Ops:
  0.6 2.0 %copy-done = f32[16,26,8,256]{3,2,1,0:T(8,128)S(1)} copy-done((f32[16,26,8,256]{3,2,1,0:T(8,128)S(1)}, f32[16,26,8,256]{3,2,1,0:T(8,128)}, u32[]{:S(2)}) %copy-start) | copy-done | bytes 3407896
  2.6 0.7 pack.1
  3.4 4.0 %collective-permute-start = (f32[8,104,256]{2,1,0:T(8,128)S(1)}, f32[8,104,256]{2,1,0:T(8,128)S(1)}, u32[]{:S(2)}, u32[]{:S(2)}) collective-permute-start(f32[8,104,256]{2,1,0:T(8,128)S(1)} %get-tuple-element.21), channel_id=1, source_target_pairs={{0,8},{8,16},{16,24},{24,32},{32,40},{40,48},{48,56},{56,64},{64,7... | collective-permute-start | bytes 2555912 | tf_op jit(solution)/shard_map/ppermute | solution.py:606
  7.4 0.0 slice-start
  7.4 0.0 slice-start.1
  7.4 1.6 %collective-permute-start.1 = (f32[8,104,256]{2,1,0:T(8,128)S(1)}, f32[8,104,256]{2,1,0:T(8,128)S(1)}, u32[]{:S(2)}, u32[]{:S(2)}) collective-permute-start(f32[8,104,256]{2,1,0:T(8,128)S(1)} %get-tuple-element.22), channel_id=1, source_target_pairs={{8,0},{16,8},{24,16},{32,24},{40,32},{48,40},{56,48},{64,56},{72,6... | collective-permute-start | bytes 2555912 | tf_op jit(solution)/shard_map/ppermute | solution.py:607
  9.0 0.0 copy-done.1
  9.0 0.0 copy-done.2
  9.0 0.0 copy-done.3
  9.0 0.0 copy-done.4
  9.0 0.0 copy-done.5
  9.0 0.0 copy-done.6
  9.0 7.4 %inside.1 = (f32[16,26,8,256]{3,2,1,0:T(8,128)S(1)}, f32[208,128]{1,0:T(8,128)S(1)}, f32[208,128]{1,0:T(8,128)S(1)}, bf16[2,208,208]{2,1,0:T(8,128)(2,1)S(1)}, bf16[2,208,208]{2,1,0:T(8,128)(2,1)S(1)}) custom-call(f32[16,26,8,256]{3,2,1,0:T(8,128)S(1)} %copy-done, f32[26,26]{1,0:T(8,128)S(1)} %copy-done.1, f32[26,26]{1,0:T(8,128)S(1)} %copy-done.2, ...), custom_call_target="tpu_custom_call" | custom-call | flops 8000000000 | bytes 7000000 | tf_op jit(solution)/shard_map/inside/pallas_call | solution.py:212
  16.4 4.0 %collective-permute-start.2 = (f32[208,128]{1,0:T(8,128)S(1)}, f32[208,128]{1,0:T(8,128)S(1)}, u32[]{:S(2)}, u32[]{:S(2)}) collective-permute-start(f32[208,128]{1,0:T(8,128)S(1)} %get-tuple-element.23), channel_id=1, source_target_pairs={{0,1},{1,2},{2,3},{3,4},{4,5},{5,6},{6,7},{8,9},{9,10},{10,11},{11... | collective-permute-start | bytes 319496 | tf_op jit(solution)/shard_map/ppermute | solution.py:612
  20.5 1.9 %collective-permute-start.3 = (f32[208,128]{1,0:T(8,128)S(1)}, f32[208,128]{1,0:T(8,128)S(1)}, u32[]{:S(2)}, u32[]{:S(2)}) collective-permute-start(f32[208,128]{1,0:T(8,128)S(1)} %get-tuple-element.24), channel_id=1, source_target_pairs={{1,0},{2,1},{3,2},{4,3},{5,4},{6,5},{7,6},{9,8},{10,9},{11,10},{12... | collective-permute-start | bytes 319496 | tf_op jit(solution)/shard_map/ppermute | solution.py:613
  22.4 3.8 %basis.1 = (f32[16,128]{1,0:T(8,128)S(1)}, bf16[26,192,256]{2,1,0:T(8,128)(2,1)S(1)}, bf16[26,192,256]{2,1,0:T(8,128)(2,1)S(1)}) custom-call(f32[24,26,8,256]{3,2,1,0:T(8,128)S(1)} %bitcast.2), custom_call_target="tpu_custom_call" | custom-call | flops 8000000000 | bytes 10000000 | tf_op jit(solution)/shard_map/basis/pallas_call | solution.py:286
  26.2 0.0 collective-permute-done.2.yb_ref
  26.2 0.6 collective-permute-done.3.ya_ref
  26.8 0.0 collective-permute-done.before
  26.8 2.3 %collective-permute-done.1.after = f32[8,104,256]{2,1,0:T(8,128)S(1)} collective-permute-done((f32[8,104,256]{2,1,0:T(8,128)S(1)}, f32[8,104,256]{2,1,0:T(8,128)S(1)}, u32[]{:S(2)}, u32[]{:S(2)}) %collective-permute-start.1) | collective-permute-done | bytes 852000 | tf_op jit(solution)/shard_map/ppermute | solution.py:607
  29.1 5.4 %halo.1 = (f32[16,26,8,256]{3,2,1,0:T(8,128)S(1)}, f32[16,16,128]{2,1,0:T(8,128)S(1)}) custom-call(f32[16,26,8,256]{3,2,1,0:T(8,128)S(1)} %get-tuple-element.18.inner, bf16[26,192,256]{2,1,0:T(8,128)(2,1)S(1)} %get-tuple-element.19.p_hi, bf16[26,192,256]{2,1,0:T(8,128)(2,1)S(1)} %get-tuple-element.20.p_lo, ...), custom_call_target="tpu_custom_call", output_to_operand_aliasing={{0}: (0, {})} | custom-call | flops 8000000000 | bytes 14000000 | tf_op jit(solution)/shard_map/halo/pallas_call | solution.py:360
  34.5 15.4 %all_to_all.10.in_ref = f32[16,16,128]{2,1,0:T(8,128)S(1)} all-to-all(f32[16,16,128]{2,1,0:T(8,128)S(1)} %get-tuple-element.28), channel_id=1, replica_groups=mesh['gx_z'=8,'gx_x'=4,'gy_y'=4,'gy_c'=2] {'gx_x','gy_y'}, dimensions={0} | all-to-all | bytes 262144 | tf_op jit(solution)/shard_map/all_to_all | solution.py:410
  50.0 20.2 %all_to_all.11.line_ref = f32[16,16,128]{2,1,0:T(8,128)S(1)} all-to-all(f32[16,16,128]{2,1,0:T(8,128)S(1)} %middle.1), channel_id=1, replica_groups=mesh['gx_z'=8,'gx_x'=4,'gy_y'=4,'gy_c'=2] {'gx_z','gy_c'}, dimensions={0} | all-to-all | bytes 262144 | tf_op jit(solution)/shard_map/all_to_all | solution.py:410
  70.1 9.1 %final.1 = (f32[16,26,8,256]{3,2,1,0:T(8,128)}, f32[16,24]{1,0:T(8,128)}, f32[16,16]{1,0:T(8,128)}) custom-call(f32[16,16,128]{2,1,0:T(8,128)S(1)} %all_to_all.11.line_ref, f32[16,26,8,256]{3,2,1,0:T(8,128)S(1)} %get-tuple-element.29.a, bf16[26,192,256]{2,1,0:T(8,128)(2,1)S(1)} %get-tuple-element.19.p_hi, bf16[26,192,256]{2,1,0:T(8,128)(2,1)S(1)} %get-tuple-element.20.p_lo), custom_call_target="tpu_custom_call" | custom-call | tf_op jit(solution)/shard_map/final/pallas_call | solution.py:572
  (13 shorter events, 0.1 us)
Async XLA Ops:
  0.6 2.0 %copy-start = (f32[16,26,8,256]{3,2,1,0:T(8,128)S(1)}, f32[16,26,8,256]{3,2,1,0:T(8,128)}, u32[]{:S(2)}) copy-start(f32[16,26,8,256]{3,2,1,0:T(8,128)} %v.1) | copy-start | bytes 10223620
  2.6 6.4 %copy-start.1 = (f32[26,26]{1,0:T(8,128)S(1)}, f32[26,26]{1,0:T(8,128)}, u32[]{:S(2)}) copy-start(f32[26,26]{1,0:T(8,128)} %along_ref.1) | copy-start | bytes 8116
  2.6 6.4 %copy-start.2 = (f32[26,26]{1,0:T(8,128)S(1)}, f32[26,26]{1,0:T(8,128)}, u32[]{:S(2)}) copy-start(f32[26,26]{1,0:T(8,128)} %across_ref.1) | copy-start | bytes 8116
  2.6 6.4 %copy-start.3 = (f32[8,256]{1,0:T(8,128)S(1)}, f32[8,256]{1,0:T(8,128)}, u32[]{:S(2)}) copy-start(f32[8,256]{1,0:T(8,128)} %coll_ref.1) | copy-start | bytes 24580
  2.6 6.4 %copy-start.4 = (s32[8,256]{1,0:T(8,128)S(1)}, s32[8,256]{1,0:T(8,128)}, u32[]{:S(2)}) copy-start(s32[8,256]{1,0:T(8,128)} %mask_ref.1) | copy-start | bytes 24580
  2.6 6.4 %copy-start.5 = (s32[8,256]{1,0:T(8,128)S(1)}, s32[8,256]{1,0:T(8,128)}, u32[]{:S(2)}) copy-start(s32[8,256]{1,0:T(8,128)} %type_ref.1) | copy-start | bytes 24580
  2.6 6.4 %copy-start.6 = (f32[4,26]{1,0:T(4,128)S(1)}, f32[4,26]{1,0:T(4,128)}, u32[]{:S(2)}) copy-start(f32[4,26]{1,0:T(4,128)} %table_ref.1) | copy-start | bytes 1252
  2.6 6.4 %copy-start.7 = (f32[26]{0:T(128)S(1)}, f32[26]{0:T(128)}, u32[]{:S(2)}) copy-start(f32[26]{0:T(128)} %rate_ref.1) | copy-start | bytes 316
  3.4 23.4 %collective-permute-start = (f32[8,104,256]{2,1,0:T(8,128)S(1)}, f32[8,104,256]{2,1,0:T(8,128)S(1)}, u32[]{:S(2)}, u32[]{:S(2)}) collective-permute-start(f32[8,104,256]{2,1,0:T(8,128)S(1)} %get-tuple-element.21), channel_id=1, source_target_pairs={{0,8},{8,16},{16,24},{24,32},{32,40},{40,48},{48,56},{56,64},{64,7... | collective-permute-start | bytes 2555912 | tf_op jit(solution)/shard_map/ppermute | solution.py:606
  7.4 15.0 %slice-start = ((s8[5111808]{0:T(1024)(128)(4,1)}), s8[4194304]{0:T(1024)(128)(4,1)S(1)}, s32[]{:S(2)}) async-start(s8[5111808]{0:T(1024)(128)(4,1)} %bitcast.1), calls=%async_computation.2 | async-start | bytes 8388608
  7.4 15.0 %slice-start.1 = ((s8[5111808]{0:T(1024)(128)(4,1)}), s8[917504]{0:T(1024)(128)(4,1)S(1)}, s32[]{:S(2)}) async-start(s8[5111808]{0:T(1024)(128)(4,1)} %bitcast.1), calls=%async_computation.3 | async-start | bytes 1835008
  7.4 21.7 %collective-permute-start.1 = (f32[8,104,256]{2,1,0:T(8,128)S(1)}, f32[8,104,256]{2,1,0:T(8,128)S(1)}, u32[]{:S(2)}, u32[]{:S(2)}) collective-permute-start(f32[8,104,256]{2,1,0:T(8,128)S(1)} %get-tuple-element.22), channel_id=1, source_target_pairs={{8,0},{16,8},{24,16},{32,24},{40,32},{48,40},{56,48},{64,56},{72,6... | collective-permute-start | bytes 2555912 | tf_op jit(solution)/shard_map/ppermute | solution.py:607
  16.4 9.8 %collective-permute-start.2 = (f32[208,128]{1,0:T(8,128)S(1)}, f32[208,128]{1,0:T(8,128)S(1)}, u32[]{:S(2)}, u32[]{:S(2)}) collective-permute-start(f32[208,128]{1,0:T(8,128)S(1)} %get-tuple-element.23), channel_id=1, source_target_pairs={{0,1},{1,2},{2,3},{3,4},{4,5},{5,6},{6,7},{8,9},{9,10},{10,11},{11... | collective-permute-start | bytes 319496 | tf_op jit(solution)/shard_map/ppermute | solution.py:612
  20.5 6.3 %collective-permute-start.3 = (f32[208,128]{1,0:T(8,128)S(1)}, f32[208,128]{1,0:T(8,128)S(1)}, u32[]{:S(2)}, u32[]{:S(2)}) collective-permute-start(f32[208,128]{1,0:T(8,128)S(1)} %get-tuple-element.24), channel_id=1, source_target_pairs={{1,0},{2,1},{3,2},{4,3},{5,4},{6,5},{7,6},{9,8},{10,9},{11,10},{12... | collective-permute-start | bytes 319496 | tf_op jit(solution)/shard_map/ppermute | solution.py:613
